TPU v7x, 32 devices: a whole 2x2x4 slice. The times are simulated.
32 devices in a mesh: grp: 2 (over core), tp: 8 (over z, y), dp: 2 (over x).
Axes of the slice: x: 2, y: 2, z: 4, core: 2. Of those that a mesh axis runs over, the one named last changes fastest.
Arguments:
- base_inputs: bfloat16 [3, 128, 8192], P(None, 'dp', ('grp', 'tp')), may hold values from -6 to 6
- small_inputs: bfloat16 [2, 3, 128, 4096], P('grp', None, 'dp', 'tp'), may hold values from -6 to 6
- base_norm_gain: float32 [8192], replicated, may hold values from 0.1 to 1.9
- base_query: bfloat16 [8192, 8192], P(None, ('grp', 'tp')), may hold values from -0.0625 to 0.0625
- base_keys_values: bfloat16 [2, 8192, 1024], P(None, None, ('grp', 'tp')), may hold values from -0.0625 to 0.0625
- base_output: bfloat16 [8192, 8192], P(('grp', 'tp')), may hold values from -0.0625 to 0.0625
- base_cache: bfloat16 [2, 128, 1024, 128], P(None, 'dp', ('grp', 'tp')), may hold values from -600 to 600
- base_final_gain: float32 [8192], replicated, may hold values from 0.1 to 1.9
- base_unembed: bfloat16 [16384, 8192], P(('grp', 'tp')), may hold values from -20 to 20
- small_norm_gain: float32 [2, 4096], P('grp'), may hold values from 0.1 to 1.9
- small_projections: bfloat16 [2, 3, 4096, 4096], P('grp', None, None, 'tp'), may hold values from -0.09375 to 0.09375
- small_output: bfloat16 [2, 4096, 4096], P('grp', 'tp'), may hold values from -0.09375 to 0.09375
- small_cache: bfloat16 [2, 2, 128, 4096, 128], P('grp', None, 'dp', 'tp'), may hold values from -600 to 600
- small_final_gain: float32 [2, 4096], P('grp'), may hold values from 0.1 to 1.9
- small_unembed: bfloat16 [2, 2, 8192, 4096], P('grp', None, 'tp'), may hold values from -0.1875 to 0.1875
- lengths: int32 [128], P('dp'), may hold values from 1 to 128, as said below
- next_tokens: int32 [3, 128], P(None, 'dp'), may hold values from 0 to 16383
Outputs:
- log_probs: float32 [3, 128, 16384], P(None, 'dp', ('grp', 'tp'))
- chosen_total: float32 [128], P('dp')
Inputs may be any that keep to these rules, and one draw needn't show every extreme that they name: `lengths`: some row holds 128 cached positions.
All inputs are finite; a program needn't handle non-finite values.
Results may differ from a plain program's by a relative error of at most 0.0035.
Values may be sent and summed in bfloat16 or wider, within the bound.
A program may use at most 256 MiB of HBM per device.

v0:
```python
import functools
import math

import jax
import jax.numpy as jnp
from jax import lax
from jax.experimental import pallas as pl
from jax.experimental.pallas import tpu as pltpu
from jax.sharding import PartitionSpec as P

HD = 128
STEPS = 3
CACHE = 128


EPSILON = 1e-05
NEGATIVE = -1e30
VMEM_LIMIT = 48 * 1024 * 1024


def partner(array, axis, bit):
    return lax.ppermute(array, axis, [(i, i ^ 1 << bit) for i in range(lax.axis_size(axis))])


def tile_of(size, most):
    tile = min(size, most)
    while size % tile:
        tile //= 2
    return tile


def rotation_tables(positions, first_pair, width, head_size):
    pair_index = (first_pair + jnp.arange(width) // 2).astype(jnp.float32)
    frequency = jnp.exp(pair_index * (-2.0 * math.log(10000.0) / head_size))
    angles = positions.astype(jnp.float32)[:, None] * frequency[None, :]
    sign = jnp.where(jnp.arange(width) % 2 == 0, -1.0, 1.0)
    return jnp.cos(angles), jnp.sin(angles) * sign


def rotate(values, cosine, sine):
    copies = values.shape[1] // cosine.shape[1]
    cosine = jnp.tile(cosine, (1, copies))
    sine = jnp.tile(sine, (1, copies))
    even = (jnp.arange(values.shape[1]) % 2 == 0)[None, :]
    other = jnp.where(even, jnp.roll(values, -1, axis=1), jnp.roll(values, 1, axis=1))
    return (values * cosine + other * sine).astype(jnp.bfloat16)


def row_scaling(x_ref):
    blocks, rows, width = x_ref.shape

    def add(index, total):
        part = x_ref[index].astype(jnp.float32)
        return total + jnp.sum(part * part, axis=-1, keepdims=True)

    total = lax.fori_loop(0, blocks, add, jnp.zeros((rows, 1), jnp.float32))
    return lax.rsqrt(total / (blocks * width) + EPSILON)


def project_kernel(weight_count, x_ref, gain_ref, *refs):
    weights = refs[:weight_count]
    outs = refs[weight_count:-1]
    scale_ref = refs[-1]
    step = pl.program_id(0)

    @pl.when(step == 0)
    def _():
        scale_ref[...] = jnp.broadcast_to(row_scaling(x_ref), scale_ref.shape)
        for out in outs:
            out[...] = jnp.zeros_like(out)

    normed = x_ref[step].astype(jnp.float32) * scale_ref[:, :1] * gain_ref[step]
    normed = normed.astype(jnp.bfloat16)
    place = 0
    for weight in weights:
        if len(weight.shape) == 2:
            outs[place][...] += jnp.dot(normed, weight[...], preferred_element_type=jnp.float32)
            place += 1
        else:
            for index in range(weight.shape[0]):
                outs[place][...] += jnp.dot(
                    normed, weight[index], preferred_element_type=jnp.float32
                )
                place += 1


def project(x, gain, weights):
    blocks, rows, tile = x.shape
    specs = []
    shapes = []
    for weight in weights:
        width = weight.shape[-1]
        lead = weight.shape[:-2]
        zeros = (0,) * len(lead)
        if weight.ndim == 4:
            specs.append(
                pl.BlockSpec((None, lead[1], tile, width), lambda k: (0, 0, k, 0))
            )
            shapes.extend([(rows, width)] * lead[1])
        elif weight.ndim == 3:
            specs.append(pl.BlockSpec((lead[0], tile, width), lambda k: (0, k, 0)))
            shapes.extend([(rows, width)] * lead[0])
        else:
            specs.append(pl.BlockSpec((tile, width), lambda k: (k, 0)))
            shapes.append((rows, width))
    return pl.pallas_call(
        functools.partial(project_kernel, len(weights)),
        grid=(blocks,),
        in_specs=[
            pl.BlockSpec((blocks, rows, tile), lambda k: (0, 0, 0)),
            pl.BlockSpec((blocks, 1, tile), lambda k: (0, 0, 0)),
        ]
        + specs,
        out_specs=[pl.BlockSpec(shape, lambda k: (0, 0)) for shape in shapes],
        out_shape=[jax.ShapeDtypeStruct(shape, jnp.float32) for shape in shapes],
        scratch_shapes=[pltpu.VMEM((rows, 128), jnp.float32)],
        compiler_params=pltpu.CompilerParams(vmem_limit_bytes=VMEM_LIMIT),
    )(x, gain.reshape(blocks, 1, tile), *weights)


def out_kernel(parts, x_ref, w_ref, o_ref):
    width = w_ref.shape[1] // parts
    for part in range(parts):
        o_ref[part] = jnp.dot(
            x_ref[...],
            w_ref[:, part * width : (part + 1) * width],
            preferred_element_type=jnp.float32,
        ).astype(o_ref.dtype)


def out_project(x, weight, blocks):
    rows, depth = x.shape
    tile = weight.shape[1] // blocks
    parts = 2 if blocks % 2 == 0 else 1
    return pl.pallas_call(
        functools.partial(out_kernel, parts),
        grid=(blocks // parts,),
        in_specs=[
            pl.BlockSpec((rows, depth), lambda n: (0, 0)),
            pl.BlockSpec((depth, tile * parts), lambda n: (0, n)),
        ],
        out_specs=pl.BlockSpec((parts, rows, tile), lambda n: (n, 0, 0)),
        out_shape=jax.ShapeDtypeStruct((blocks, rows, tile), jnp.bfloat16),
        compiler_params=pltpu.CompilerParams(vmem_limit_bytes=VMEM_LIMIT),
    )(x, weight)


def logit_kernel(x_ref, gain_ref, w_ref, o_ref, normed_ref):
    blocks, rows, width = x_ref.shape

    @pl.when((pl.program_id(0) == 0) & (pl.program_id(1) == 0))
    def _():
        scaling = row_scaling(x_ref)

        def fill(index, carry):
            normed = x_ref[index].astype(jnp.float32) * scaling * gain_ref[index]
            columns = pl.ds(pl.multiple_of(index * width, width), width)
            normed_ref[:, columns] = normed.astype(jnp.bfloat16)
            return carry

        lax.fori_loop(0, blocks, fill, 0)

    o_ref[...] = lax.dot_general(
        normed_ref[...], w_ref[...], (((1,), (1,)), ((), ())), preferred_element_type=jnp.float32
    )


def logit_project(x, gain, table, most):
    blocks, rows, block_width = x.shape
    depth = blocks * block_width
    parts, width = table.shape[:2]
    tile = tile_of(width, most)
    return pl.pallas_call(
        logit_kernel,
        grid=(parts, width // tile),
        in_specs=[
            pl.BlockSpec((blocks, rows, block_width), lambda p, n: (0, 0, 0)),
            pl.BlockSpec((blocks, 1, block_width), lambda p, n: (0, 0, 0)),
            pl.BlockSpec((None, tile, depth), lambda p, n: (p, n, 0)),
        ],
        out_specs=pl.BlockSpec((None, rows, tile), lambda p, n: (p, 0, n)),
        out_shape=jax.ShapeDtypeStruct((parts, rows, width), jnp.float32),
        scratch_shapes=[pltpu.VMEM((rows, depth), jnp.bfloat16)],
        compiler_params=pltpu.CompilerParams(vmem_limit_bytes=VMEM_LIMIT),
    )(x, gain.reshape(blocks, 1, block_width), table)


def attention_weights(cached_scores, fresh_scores, visible, causal):
    factor = 1.0 / math.sqrt(HD)
    cached_scores = jnp.where(visible, cached_scores * factor, NEGATIVE)
    fresh_scores = jnp.where(causal, fresh_scores * factor, NEGATIVE)
    row_max = jnp.maximum(
        jnp.max(cached_scores, axis=-1, keepdims=True),
        jnp.max(fresh_scores, axis=-1, keepdims=True),
    )
    cached_exp = jnp.exp(cached_scores - row_max)
    fresh_exp = jnp.exp(fresh_scores - row_max)
    totals = jnp.sum(cached_exp, axis=-1, keepdims=True) + jnp.sum(
        fresh_exp, axis=-1, keepdims=True
    )
    return ((cached_exp / totals).astype(jnp.bfloat16), (fresh_exp / totals).astype(jnp.bfloat16))


def flips(index, bits):
    return [bit * (1 - 2 * (lax.div(index, bit) % 2)) for bit in bits]


def span(offsets):
    sums = [0]
    for offset in offsets:
        sums = sums + [total + offset for total in sums]
    return sums


def link_order(size, group):
    count = size.bit_length() - 1
    first = list(reversed(range(count)))
    second = [0] + list(reversed(range(1, count))) if count else []
    return [(1 << a) + group * ((1 << b) - (1 << a)) for a, b in zip(first, second)]


def greet(partners):
    barrier = pltpu.get_barrier_semaphore()
    for target in partners:
        pl.semaphore_signal(
            barrier, inc=1, device_id=target, device_id_type=pl.DeviceIdType.MESH
        )
    pl.semaphore_wait(barrier, len(partners))


def send(source, target, sends, receives, place, device):
    copy = pltpu.make_async_remote_copy(
        src_ref=source,
        dst_ref=target,
        send_sem=sends.at[place],
        recv_sem=receives.at[place],
        device_id=device,
        device_id_type=pl.DeviceIdType.MESH,
    )
    copy.start()
    return copy


def gather_kernel(size, x_ref, o_ref, local_sem, sends, receives, core_sends, core_receives):
    group = lax.axis_index("grp")
    mine = lax.axis_index("tp")
    data = lax.axis_index("dp")
    offsets = flips(mine, link_order(size, group))
    other_core = (1 - group, mine, data)
    greet([(group, mine + offset, data) for offset in offsets] + [other_core])
    base = group * size
    keep = pltpu.make_async_copy(x_ref, o_ref.at[base + mine], local_sem)
    keep.start()
    keep.wait()
    held = [0]
    place = 0
    waiting = []
    swaps = [
        send(o_ref.at[base + mine], o_ref.at[base + mine], core_sends, core_receives, 0, other_core)
    ]
    for offset in offsets:
        copies = []
        for inner in held:
            block = base + mine + inner
            copies.append(
                send(
                    o_ref.at[block],
                    o_ref.at[block],
                    sends,
                    receives,
                    place,
                    (group, mine + offset, data),
                )
            )
            place += 1
        arrived = [inner + offset for inner in held]
        for copy, inner in zip(copies, arrived):
            copy.wait_recv()
            block = base + mine + inner
            swaps.append(
                send(
                    o_ref.at[block],
                    o_ref.at[block],
                    core_sends,
                    core_receives,
                    len(swaps),
                    other_core,
                )
            )
        waiting.extend(copies)
        held = held + arrived
    for copy in waiting:
        copy.wait_send()
    for copy in swaps:
        copy.wait()


def gather_blocks(block, identity):
    size = lax.axis_size("tp")
    count = lax.axis_size("grp") * size
    return pl.pallas_call(
        functools.partial(gather_kernel, size),
        in_specs=[pl.BlockSpec(memory_space=pltpu.VMEM)],
        out_specs=pl.BlockSpec(memory_space=pltpu.VMEM),
        out_shape=jax.ShapeDtypeStruct((count,) + block.shape, block.dtype),
        scratch_shapes=[
            pltpu.SemaphoreType.DMA(()),
            pltpu.SemaphoreType.DMA((size,)),
            pltpu.SemaphoreType.DMA((size,)),
            pltpu.SemaphoreType.DMA((size,)),
            pltpu.SemaphoreType.DMA((size,)),
        ],
        compiler_params=pltpu.CompilerParams(
            collective_id=identity, has_side_effects=True, vmem_limit_bytes=VMEM_LIMIT
        ),
    )(block)


def scatter_kernel(
    size, p_ref, x_ref, o_ref, total, stage, core_box, box, core_sends, core_receives, sends, receives
):
    group = lax.axis_index("grp")
    mine = lax.axis_index("tp")
    data = lax.axis_index("dp")
    offsets = flips(mine, list(reversed(link_order(size, group))))
    other_core = (1 - group, mine, data)
    greet([(group, mine + offset, data) for offset in offsets] + [other_core])
    order = list(reversed(span(list(reversed(offsets)))))
    swaps = [
        send(
            p_ref.at[(1 - group) * size + mine + inner_other],
            core_box.at[place],
            core_sends,
            core_receives,
            place,
            other_core,
        )
        for place, inner_other in enumerate(
            list(reversed(span(list(reversed(other_offsets(size, group, mine))))))
        )
    ]
    copies = []
    place = 0
    half = size // 2
    for index, inner in enumerate(order):
        swaps[index].wait_recv()
        value = p_ref[group * size + mine + inner].astype(jnp.float32)
        value = value + core_box[index].astype(jnp.float32)
        total[index] = value
        if size > 1 and index < half:
            stage[index] = value.astype(stage.dtype)
            copies.append(
                send(
                    stage.at[index],
                    box.at[place],
                    sends,
                    receives,
                    place,
                    (group, mine + offsets[0], data),
                )
            )
            place += 1
    first = half
    start = 0
    for phase in range(len(offsets)):
        active = size - first
        for index in range(active):
            copies[start + index].wait_recv()
            value = total[first + index] + box[start + index].astype(jnp.float32)
            total[first + index] = value
            if active > 1 and index < active // 2:
                stage[first + index] = value.astype(stage.dtype)
                copies.append(
                    send(
                        stage.at[first + index],
                        box.at[place],
                        sends,
                        receives,
                        place,
                        (group, mine + offsets[phase + 1], data),
                    )
                )
                place += 1
        start += active
        first += active // 2
    hidden = x_ref[...].astype(jnp.float32) + total[size - 1]
    o_ref[...] = hidden.astype(o_ref.dtype)
    for copy in copies + swaps:
        copy.wait_send()


def other_offsets(size, group, mine):
    return flips(mine, list(reversed(link_order(size, 1 - group))))


def scatter_blocks(partial, inputs, identity):
    size = lax.axis_size("tp")
    block = inputs.shape
    whole = pl.BlockSpec(memory_space=pltpu.VMEM)
    return pl.pallas_call(
        functools.partial(scatter_kernel, size),
        in_specs=[whole, whole],
        out_specs=whole,
        out_shape=jax.ShapeDtypeStruct(block, inputs.dtype),
        scratch_shapes=[
            pltpu.VMEM((size,) + block, jnp.float32),
            pltpu.VMEM((size,) + block, partial.dtype),
            pltpu.VMEM((size,) + block, partial.dtype),
            pltpu.VMEM((size,) + block, partial.dtype),
            pltpu.SemaphoreType.DMA((size,)),
            pltpu.SemaphoreType.DMA((size,)),
            pltpu.SemaphoreType.DMA((size,)),
            pltpu.SemaphoreType.DMA((size,)),
        ],
        compiler_params=pltpu.CompilerParams(
            collective_id=identity, has_side_effects=True, vmem_limit_bytes=VMEM_LIMIT
        ),
    )(partial, inputs)


def share_kernel(size, count, x_ref, o_ref, sends, receives):
    data = lax.axis_index("dp")
    mine = lax.axis_index("grp") * size + lax.axis_index("tp")
    others = [(mine + step) % count for step in range(1, count)]
    devices = [(other // size, other % size, data) for other in others]
    greet(devices)
    copies = [
        send(x_ref, o_ref.at[mine], sends, receives, place, device)
        for place, device in enumerate(devices)
    ]
    o_ref[mine] = x_ref[...]
    for copy in copies:
        copy.wait()


def share_small(values, identity):
    size = lax.axis_size("tp")
    count = lax.axis_size("grp") * size
    whole = pl.BlockSpec(memory_space=pltpu.VMEM)
    return pl.pallas_call(
        functools.partial(share_kernel, size, count),
        in_specs=[whole],
        out_specs=whole,
        out_shape=jax.ShapeDtypeStruct((count,) + values.shape, values.dtype),
        scratch_shapes=[
            pltpu.SemaphoreType.DMA((count - 1,)),
            pltpu.SemaphoreType.DMA((count - 1,)),
        ],
        compiler_params=pltpu.CompilerParams(collective_id=identity, has_side_effects=True),
    )(values)


def body(
    base_inputs,
    small_inputs,
    base_norm_gain,
    base_query,
    base_keys_values,
    base_output,
    base_cache,
    base_final_gain,
    base_unembed,
    small_norm_gain,
    small_projections,
    small_output,
    small_cache,
    small_final_gain,
    small_unembed,
    lengths,
    next_tokens,
):
    row_count = lengths.shape[0]
    total_rows = STEPS * row_count
    slice_width = base_keys_values.shape[2]
    share_count = HD // slice_width
    group_size = base_query.shape[1] // slice_width
    slice_index = lax.axis_index("tp") % share_count
    first_pair = slice_index * (slice_width // 2)
    block_index = lax.axis_index("grp") * lax.axis_size("tp") + lax.axis_index("tp")
    vocab_width = base_unembed.shape[0]
    small_heads = small_projections.shape[3] // HD
    small_block = small_inputs.reshape(total_rows, -1)
    base_block = base_inputs.reshape(total_rows, -1)
    small_full = lax.all_gather(small_block, "tp", axis=0)
    base_full = gather_blocks(base_block, 0)
    positions = (jnp.arange(STEPS)[:, None] + lengths[None, :]).reshape(-1)
    visible = (jnp.arange(CACHE)[None, :] < lengths[:, None])[:, None, None, :]
    step_range = jnp.arange(STEPS)
    causal = step_range[None, :] <= step_range[:, None]

    small_q, small_k, small_v = project(
        small_full, small_norm_gain, [small_projections]
    )
    cosine, sine = rotation_tables(positions, 0, HD, HD)
    by_head = (STEPS, row_count, small_heads, HD)
    small_q = rotate(small_q, cosine, sine).reshape(by_head)
    small_k = rotate(small_k, cosine, sine).reshape(by_head)
    small_v = small_v.astype(jnp.bfloat16).reshape(by_head)
    keys = small_cache[0, 0].reshape(row_count, small_heads, HD, CACHE)
    values = small_cache[0, 1].reshape(row_count, small_heads, HD, CACHE)
    cached = jnp.einsum("srhd,rhdl->rhsl", small_q, keys, preferred_element_type=jnp.float32)
    fresh = jnp.einsum("srhd,nrhd->rhsn", small_q, small_k, preferred_element_type=jnp.float32)
    cached, fresh = attention_weights(cached, fresh, visible, causal[None, None])
    heads = jnp.einsum("rhsl,rhdl->srhd", cached, values, preferred_element_type=jnp.float32)
    heads = heads + jnp.einsum(
        "rhsn,nrhd->srhd", fresh, small_v, preferred_element_type=jnp.float32
    )
    heads = heads.astype(jnp.bfloat16).reshape(total_rows, small_heads * HD)
    small_partial = out_project(heads, small_output[0], small_full.shape[0])
    small_mixed = lax.psum_scatter(small_partial, "tp", scatter_dimension=0, tiled=False)
    small_hidden = small_block.astype(jnp.float32) + small_mixed.astype(jnp.float32)
    small_hidden = lax.all_gather(small_hidden.astype(jnp.bfloat16), "tp", axis=0)
    small_logits = logit_project(small_hidden, small_final_gain, small_unembed[0], 512)
    group = lax.axis_index("grp")
    own = lax.dynamic_index_in_dim(small_logits, group, 0, keepdims=False)
    theirs = lax.dynamic_index_in_dim(small_logits, 1 - group, 0, keepdims=False)
    received = lax.ppermute(theirs, "grp", [(0, 1), (1, 0)])

    query, new_key, new_value = project(
        base_full, base_norm_gain, [base_query, base_keys_values]
    )
    cosine, sine = rotation_tables(positions, first_pair, slice_width, HD)
    query = rotate(query, cosine, sine).reshape(STEPS, row_count, group_size, slice_width)
    new_key = rotate(new_key, cosine, sine).reshape(STEPS, row_count, slice_width)
    new_value = new_value.astype(jnp.bfloat16).reshape(STEPS, row_count, slice_width)
    cached = jnp.einsum("srgd,rdl->rsgl", query, base_cache[0], preferred_element_type=jnp.float32)
    fresh = jnp.einsum("srgd,nrd->rsgn", query, new_key, preferred_element_type=jnp.float32)
    for bit in range(share_count.bit_length() - 1):
        cached = cached + partner(cached, "tp", bit)
        fresh_flat = fresh.reshape(row_count, -1)
        fresh = fresh + partner(fresh_flat, "tp", bit).reshape(fresh.shape)
    cached, fresh = attention_weights(cached, fresh, visible, causal[:, None, :][None])
    heads = jnp.einsum("rsgl,rdl->srgd", cached, base_cache[1], preferred_element_type=jnp.float32)
    heads = heads + jnp.einsum(
        "rsgn,nrd->srgd", fresh, new_value, preferred_element_type=jnp.float32
    )
    heads = heads.astype(jnp.bfloat16).reshape(total_rows, group_size * slice_width)
    partial = out_project(heads, base_output, base_full.shape[0])
    hidden = gather_blocks(scatter_blocks(partial, base_block, 1), 2)
    base_logits = logit_project(hidden, base_final_gain, base_unembed[None], 256)[0]
    gap = jnp.where(group == 0, own - received, received - own)
    steered = base_logits + gap

    local_max = jnp.max(steered, axis=-1)
    local_total = jnp.sum(jnp.exp(steered - local_max[:, None]), axis=-1)
    token_local = next_tokens.reshape(-1) - block_index * vocab_width
    token_hit = jnp.arange(vocab_width)[None, :] == token_local[:, None]
    picked = jnp.sum(jnp.where(token_hit, steered, 0.0), axis=-1)
    packed = jnp.stack([local_max, local_total, picked])
    packed = jnp.pad(packed, ((0, -3 % 8), (0, -total_rows % 128)))
    stats = share_small(packed, 3)[:, :3, :total_rows]
    row_max = jnp.max(stats[:, 0], axis=0)
    exp_total = jnp.sum(stats[:, 1] * jnp.exp(stats[:, 0] - row_max[None]), axis=0)
    log_norm = row_max + jnp.log(exp_total)
    chosen = jnp.sum(stats[:, 2], axis=0) - log_norm
    log_probs = steered - log_norm[:, None]
    return (
        log_probs.reshape(STEPS, row_count, vocab_width),
        jnp.sum(chosen.reshape(STEPS, row_count), axis=0),
    )


def solution(mesh):
    placed = (
        P(None, "dp", ("grp", "tp")),
        P("grp", None, "dp", "tp"),
        P(),
        P(None, ("grp", "tp")),
        P(None, None, ("grp", "tp")),
        P(("grp", "tp"), None),
        P(None, "dp", ("grp", "tp"), None),
        P(),
        P(("grp", "tp"), None),
        P("grp", None),
        P("grp", None, None, "tp"),
        P("grp", "tp", None),
        P("grp", None, "dp", "tp", None),
        P("grp", None),
        P("grp", None, "tp", None),
        P("dp"),
        P(None, "dp"),
    )
    return jax.shard_map(
        body,
        mesh=mesh,
        in_specs=placed,
        out_specs=(P(None, "dp", ("grp", "tp")), P("dp")),
        check_vma=False,
    )
```

profile of v0, /device:TPU:0, one launch (start us, length us, event | category | flops | bytes accessed | tf_op | source)
XLA Modules:
  0.0 322.9 jit_solution(7284579677675783676)
XLA Ops:
  7.2 0.7 all-gather.3.cloned.1.call-update
  7.9 0.7 add_convert_fusion.1
  8.7 0.7 iota_compare_fusion.1
  9.9 11.7 %fusion.66 = (bf16[1,1,64,512,128]{4,3,2,1,0:T(8,128)(2,1)}, bf16[1,1,64,512,128]{4,3,2,1,0:T(8,128)(2,1)}) fusion(bf16[1,2,64,512,128]{4,3,2,1,0:T(8,128)(2,1)} %param.29), kind=kLoop, calls=%fused_computation.128 | loop fusion | bytes 33554432 | tf_op jit(solution)/shard_map/slice | solution.py:500
  21.6 35.5 %all-gather.3.cloned.1.call-done.x_ref = bf16[8,192,512]{2,1,0:T(8,128)(2,1)} async-done(((bf16[1,192,512]{2,1,0:T(8,128)(2,1)}), bf16[8,192,512]{2,1,0:T(8,128)(2,1)}) %all-gather.3.cloned.1.call-update) | async-done | bytes 1572880 | tf_op jit(solution)/shard_map/all_gather | solution.py:484
  57.1 1.4 copy-done.3
  58.5 9.7 %shard_map.182 = (f32[192,512]{1,0:T(8,128)S(1)}, f32[192,512]{1,0:T(8,128)S(1)}, f32[192,512]{1,0:T(8,128)S(1)}) custom-call(bf16[8,192,512]{2,1,0:T(8,128)(2,1)S(1)} %copy-done.3, f32[8,1,512]{2,1,0:T(1,128)S(1)} %bitcast.119, bf16[1,3,4096,512]{3,2,1,0:T(8,128)(2,1)} %refs_0_.3), custom_call_target="tpu_custom_call" | custom-call | tf_op jit(solution)/shard_map/pallas_call | solution.py:106
  70.2 5.8 %fusion.75 = (f32[64,4,3]{2,1,0:T(4,128)S(1)}, f32[64,4,3,128]{3,2,1,0:T(4,128)S(1)}) fusion(bf16[64,4,128,128]{3,2,1,0:T(8,128)(2,1)} %bitcast.121, bf16[3,64,4,128]{3,2,1,0:T(4,128)(2,1)S(1)} %reshape.395, pred[64,128]{1,0:T(8,128)(4,1)S(1)} %iota_compare_fusion.1), kind=kOutput, calls=%fused_computation.137 | convolution fusion | flops 25459968 | bytes 8989696 | tf_op jit(solution)/shard_map/srhd,rhdl->rhsl/dot_general | solution.py:501
  76.1 0.8 fusion.13
  78.2 8.1 %fusion.4 = bf16[3,64,4,128]{3,0,2,1:T(4,128)(2,1)S(1)} fusion(f32[3,64,4,128]{3,0,2,1:T(4,128)S(1)} %convolution_bitcast_fusion.2, bf16[64,4,128,128]{3,2,1,0:T(8,128)(2,1)} %bitcast.124, f32[64,4,3,128]{3,2,1,0:T(4,128)S(1)} %get-tuple-element.54, f32[64,4,3]{2,1,0:T(4,128)S(1)} %add.176, f32[64,4,3]{2,1,0:T(4,128)S(1)} %max.17), kind=kOutput, calls=%fused_computation.9 | convolution fusion | flops 25657344 | bytes 9377792 | tf_op jit(solution)/shard_map/rhsl,rhdl->srhd/dot_general | solution.py:504
  86.4 2.9 shard_map.183
  89.6 41.6 %shard_map.176.x_ref = bf16[16,192,512]{2,1,0:T(8,128)(2,1)S(1)} custom-call(bf16[192,512]{1,0:T(8,128)(2,1)S(1)} %bitcast.115), custom_call_target="tpu_custom_call" | custom-call | tf_op jit(solution)/shard_map/pallas_call | solution.py:301
  131.3 4.8 %copy.137.refs_1_ = bf16[2,8192,64]{2,1,0:T(8,128)(2,1)} copy(bf16[2,8192,64]{1,2,0:T(8,128)(2,1)} %param.21) | data formatting | bytes 4194304 | tf_op args[4]
  136.1 0.8 copy-done.8
  136.8 15.0 %shard_map.177 = (f32[192,512]{1,0:T(8,128)S(1)}, f32[192,64]{1,0:T(8,128)S(1)}, f32[192,64]{1,0:T(8,128)S(1)}) custom-call(bf16[16,192,512]{2,1,0:T(8,128)(2,1)S(1)} %shard_map.176.x_ref, f32[16,1,512]{2,1,0:T(1,128)S(1)} %bitcast.117, bf16[8192,512]{1,0:T(8,128)(2,1)} %refs_0_.2, bf16[2,8192,64]{2,1,0:T(8,128)(2,1)} %copy.137.refs_1_), custom_call_target="tpu_custom_call" | custom-call | tf_op jit(solution)/shard_map/pallas_call | solution.py:106
  151.9 0.6 copy-done.1
  152.5 0.6 copy-done.6
  153.2 7.0 %reduce-scatter.2.cloned.1.call-done = bf16[1,192,512]{2,1,0:T(8,128)(2,1)} async-done(((bf16[8,192,512]{2,1,0:T(8,128)(2,1)}), bf16[1,192,512]{2,1,0:T(8,128)(2,1)}) %reduce-scatter.2.cloned.1.call-update) | async-done | bytes 196624 | tf_op jit(solution)/shard_map/reduce_scatter | solution.py:510
  160.2 1.7 add_convert_fusion
  161.9 1.1 fusion.74
  163.0 1.1 fusion.67
  164.1 1.3 fusion.40
  166.7 1.6 fusion.6
  168.3 1.1 collective-permute-start
  169.4 1.3 fusion.23
  170.9 1.1 collective-permute-start.1
  172.1 0.6 convert_element_type.87
  172.7 0.6 sub.114
  173.3 16.1 %collective-permute-done.1 = f32[64,72]{0,1:T(8,128)S(1)} collective-permute-done((f32[64,72]{0,1:T(8,128)S(1)}, f32[64,72]{0,1:T(8,128)S(1)}, u32[]{:S(2)}, u32[]{:S(2)}) %collective-permute-start.1) | collective-permute-done | bytes 18464 | tf_op jit(solution)/shard_map/ppermute | solution.py:22
  189.7 0.5 fusion.64
  190.1 1.5 fusion.65
  191.6 0.6 fusion.12
  192.2 15.7 %all-gather.5.cloned.1.call-done.x_ref = bf16[8,192,512]{2,1,0:T(8,128)(2,1)} async-done(((bf16[1,192,512]{2,1,0:T(8,128)(2,1)}), bf16[8,192,512]{2,1,0:T(8,128)(2,1)}) %all-gather.5.cloned.1.call-update) | async-done | bytes 1572880 | tf_op jit(solution)/shard_map/all_gather | solution.py:512
  207.9 1.4 copy-done.2
  209.3 10.7 %shard_map.184 = f32[2,192,1024]{2,1,0:T(8,128)S(1)} custom-call(bf16[8,192,512]{2,1,0:T(8,128)(2,1)S(1)} %copy-done.2, f32[8,1,512]{2,1,0:T(1,128)S(1)} %bitcast.120, bf16[2,1024,4096]{2,1,0:T(8,128)(2,1)} %bitcast.123), custom_call_target="tpu_custom_call" | custom-call | tf_op jit(solution)/shard_map/pallas_call | solution.py:173
  220.0 0.9 dynamic-slice_bitcast_fusion
  221.4 0.4 convolution_bitcast_fusion.1
  221.8 0.7 fusion.1
  222.9 7.1 %shard_map.178.p_ref = bf16[16,192,512]{2,1,0:T(8,128)(2,1)S(1)} custom-call(bf16[192,512]{1,0:T(8,128)(2,1)S(1)} %reshape.391.x_ref, bf16[512,8192]{1,0:T(8,128)(2,1)} %w_ref.1), custom_call_target="tpu_custom_call" | custom-call | tf_op jit(solution)/shard_map/pallas_call | solution.py:135
  230.1 26.6 %shard_map.179.x_ref = bf16[192,512]{1,0:T(8,128)(2,1)S(1)} custom-call(bf16[16,192,512]{2,1,0:T(8,128)(2,1)S(1)} %shard_map.178.p_ref, bf16[192,512]{1,0:T(8,128)(2,1)S(1)} %bitcast.116), custom_call_target="tpu_custom_call" | custom-call | tf_op jit(solution)/shard_map/pallas_call | solution.py:400
  256.6 28.9 %shard_map.180.x_ref = bf16[16,192,512]{2,1,0:T(8,128)(2,1)S(1)} custom-call(bf16[192,512]{1,0:T(8,128)(2,1)S(1)} %shard_map.179.x_ref), custom_call_target="tpu_custom_call" | custom-call | tf_op jit(solution)/shard_map/pallas_call | solution.py:301
  285.6 11.9 %shard_map.181 = f32[1,192,1024]{2,1,0:T(8,128)S(1)} custom-call(bf16[16,192,512]{2,1,0:T(8,128)(2,1)S(1)} %shard_map.180.x_ref, f32[16,1,512]{2,1,0:T(1,128)S(1)} %bitcast.118, bf16[1,1024,8192]{2,1,0:T(8,128)(2,1)} %bitcast.122), custom_call_target="tpu_custom_call" | custom-call | tf_op jit(solution)/shard_map/pallas_call | solution.py:173
  297.5 1.4 fusion.62
  299.2 0.6 select_maximum_fusion.x_ref
  299.8 13.8 %shard_map.185 = f32[16,8,256]{2,1,0:T(8,128)} custom-call(f32[8,256]{1,0:T(8,128)} %select_maximum_fusion.x_ref), custom_call_target="tpu_custom_call" | custom-call | tf_op jit(solution)/shard_map/pallas_call | solution.py:440
  313.6 1.1 slice_reduce_fusion
  314.7 1.0 broadcast_subtract_fusion
  315.8 0.5 reduce_sum.89
  (95 shorter events, 7.3 us)
Async XLA Ops:
  7.2 49.9 %all-gather.3.cloned.1.call-start = ((), (), s32[]{:S(2)}) async-start(), calls=%async_computation.1 | async-start | bytes 1769472 | tf_op jit(solution)/shard_map/all_gather | solution.py:484
  7.9 152.3 %reduce-scatter.2.cloned.1.call-start = ((), (), s32[]{:S(2)}) async-start(), calls=%async_computation.2 | async-start | bytes 1769472 | tf_op jit(solution)/shard_map/reduce_scatter | solution.py:510
  8.7 68.6 %copy-start.15 = (pred[3,3]{1,0:T(4,128)(4,1)}, pred[3,3]{1,0:T(4,128)(4,1)S(1)}, u32[]{:S(2)}) copy-start(pred[3,3]{1,0:T(4,128)(4,1)S(1)} %iota_compare_fusion.4) | copy-start | bytes 31
  9.5 60.7 %copy-start.13 = (pred[64,128]{1,0:T(8,128)(4,1)}, pred[64,128]{1,0:T(8,128)(4,1)S(1)}, u32[]{:S(2)}) copy-start(pred[64,128]{1,0:T(8,128)(4,1)S(1)} %iota_compare_fusion.1) | copy-start | bytes 24580
  9.9 47.2 %copy-start.10 = (f32[1,4096]{1,0:T(1,128)S(1)}, f32[1,4096]{1,0:T(1,128)}, u32[]{:S(2)}) copy-start(f32[1,4096]{1,0:T(1,128)} %param.26) | copy-start | bytes 49156
  57.1 1.4 copy-start.3
  77.8 8.7 %copy-start = (bf16[1,512,4096]{2,1,0:T(8,128)(2,1)S(1)}, bf16[1,512,4096]{2,1,0:T(8,128)(2,1)}, u32[]{:S(2)}) copy-start(bf16[1,512,4096]{2,1,0:T(8,128)(2,1)} %param.28) | copy-start | bytes 12582916
  78.2 11.4 %copy-start.4 = (bf16[3,64,512]{2,1,0:T(8,128)(2,1)S(1)}, bf16[3,64,512]{2,1,0:T(8,128)(2,1)}, u32[]{:S(2)}) copy-start(bf16[3,64,512]{2,1,0:T(8,128)(2,1)} %param.17) | copy-start | bytes 589828
  89.4 118.5 %all-gather.5.cloned.1.call-start = ((), (), s32[]{:S(2)}) async-start(), calls=%async_computation.3 | async-start | bytes 1769472 | tf_op jit(solution)/shard_map/all_gather | solution.py:512
  136.1 0.8 copy-start.8
  151.9 0.6 copy-start.1
  152.5 0.6 copy-start.6
  153.1 18.9 %copy-start.18 = (s32[3,64]{1,0:T(4,128)S(1)}, s32[3,64]{1,0:T(4,128)}, u32[]{:S(2)}) copy-start(s32[3,64]{1,0:T(4,128)} %param.33) | copy-start | bytes 2308
  153.2 36.5 %copy-start.16 = (pred[3,3]{1,0:T(4,128)(4,1)S(1)}, pred[3,3]{1,0:T(4,128)(4,1)}, u32[]{:S(2)}) copy-start(pred[3,3]{1,0:T(4,128)(4,1)} %copy-done.15) | copy-start | bytes 31
  153.2 18.9 %copy-start.7 = (f32[192,64]{1,0:T(8,128)S(1)}, f32[192,64]{1,0:T(8,128)}, u32[]{:S(2)}) copy-start(f32[192,64]{1,0:T(8,128)} %copy-done.6) | copy-start | bytes 147460
  165.6 42.3 %copy-start.11 = (f32[1,4096]{1,0:T(1,128)S(1)}, f32[1,4096]{1,0:T(1,128)}, u32[]{:S(2)}) copy-start(f32[1,4096]{1,0:T(1,128)} %param.30) | copy-start | bytes 49156
  168.3 21.8 %collective-permute-start = (f32[64,3,8,128]{3,2,1,0:T(8,128)S(1)}, f32[64,3,8,128]{3,2,1,0:T(8,128)}, u32[]{:S(2)}, u32[]{:S(2)}) collective-permute-start(f32[64,3,8,128]{3,2,1,0:T(8,128)S(1)} %fusion.6), channel_id=1, source_target_pairs={{0,2},{2,0},{4,6},{6,4},{8,10},{10,8},{12,14},{14,12},{1,3},{3,1},... | collective-permute-start | bytes 2359304 | tf_op jit(solution)/shard_map/ppermute | solution.py:22
  170.9 18.5 %collective-permute-start.1 = (f32[64,72]{0,1:T(8,128)S(1)}, f32[64,72]{0,1:T(8,128)S(1)}, u32[]{:S(2)}, u32[]{:S(2)}) collective-permute-start(f32[64,72]{0,1:T(8,128)S(1)} %reshape.388), channel_id=1, source_target_pairs={{0,2},{2,0},{4,6},{6,4},{8,10},{10,8},{12,14},{14,12},{1,3},{3,1},... | collective-permute-start | bytes 55304 | tf_op jit(solution)/shard_map/ppermute | solution.py:22
  207.9 1.4 copy-start.2
  209.3 12.1 %copy-start.14 = (bf16[192,64]{1,0:T(8,128)(2,1)S(1)}, bf16[192,64]{1,0:T(8,128)(2,1)}, u32[]{:S(2)}) copy-start(bf16[192,64]{1,0:T(8,128)(2,1)} %convert_element_type.87) | copy-start | bytes 73732
  209.3 12.5 %copy-start.12 = (bf16[2,64,64,128]{3,2,1,0:T(8,128)(2,1)S(1)}, bf16[2,64,64,128]{3,2,1,0:T(8,128)(2,1)}, u32[]{:S(2)}) copy-start(bf16[2,64,64,128]{3,2,1,0:T(8,128)(2,1)} %param.23) | copy-start | bytes 6291460
  221.0 76.5 %collective-permute-start.2 = (f32[192,1024]{1,0:T(8,128)}, f32[192,1024]{1,0:T(8,128)}, u32[]{:S(2)}, u32[]{:S(2)}) collective-permute-start(f32[192,1024]{1,0:T(8,128)} %dynamic-slice_bitcast_fusion), channel_id=1, source_target_pairs={{0,16},{16,0},{1,17},{17,1},{2,18},{18,2},{3,19},{19,3},{4,20},{20... | collective-permute-start | bytes 2359304 | tf_op jit(solution)/shard_map/ppermute | solution.py:517
  222.6 7.5 %copy-start.5 = (bf16[3,64,512]{2,1,0:T(8,128)(2,1)S(1)}, bf16[3,64,512]{2,1,0:T(8,128)(2,1)}, u32[]{:S(2)}) copy-start(bf16[3,64,512]{2,1,0:T(8,128)(2,1)} %param.17) | copy-start | bytes 589828
  222.9 62.7 %copy-start.9 = (f32[8192]{0:T(1024)S(1)}, f32[8192]{0:T(1024)}, u32[]{:S(2)}) copy-start(f32[8192]{0:T(1024)} %param.24) | copy-start | bytes 98308
  285.6 13.2 %copy-start.17 = (s32[192]{0:T(256)S(1)}, s32[192]{0:T(256)}, u32[]{:S(2)}) copy-start(s32[192]{0:T(256)} %sub.114) | copy-start | bytes 2308
Sparse Core Ops, SparseCore 0:
  10.2 46.8 all-gather.2
  89.5 70.6 reduce-scatter.1
  163.2 44.6 all-gather.4
where the time goes:
time: 324 us; the launch traced here: 323 us
  Pallas kernels  168 us (52%)
  waiting for transfers between devices  74.9 us (23%)
  local copies, waits for them, and re-layouts  28.8 us (9%)
  matrix products  18.8 us (6%)
  other arithmetic  15.3 us (5%)
  between operations  14.3 us (4%)
    pallas_call x2, Pallas kernels, gather_blocks(): pl.pallas_call(functools.partial(gather_kernel, size), in_specs=[pl.Block...  70.6 us
    all_gather x1, waiting for transfers between devices, body(): small_full = lax.all_gather(small_block, 'tp', axis=0)  35.5 us
    pallas_call x1, Pallas kernels, scatter_blocks(): pl.pallas_call(functools.partial(scatter_kernel, size), in_specs=[whole,...  26.6 us
    pallas_call x2, Pallas kernels, project(): pl.pallas_call(functools.partial(project_kernel, len(weights)), grid=(blo...  24.7 us
    pallas_call x2, Pallas kernels, logit_project(): pl.pallas_call(logit_kernel, grid=(parts, width // tile), in_specs=[pl.Bl...  22.6 us
    ppermute x2, waiting for transfers between devices, partner(): lax.ppermute(array, axis, [(i, i ^ 1 << bit) for i in range(lax.axis_size...  16.1 us
    all_gather x1, waiting for transfers between devices, body(): lax.all_gather(small_hidden.astype(jnp.bfloat16), 'tp', axis=0)  15.7 us
    pallas_call x1, Pallas kernels, share_small(): pl.pallas_call(functools.partial(share_kernel, size, count), in_specs=[wh...  13.8 us
  transfers between devices with their start and end apart: 6, of which 4 were waited for; matrix products, arithmetic and copies ran while one was open for 10% of the time, Pallas kernels for 41%

commit v1 on v0

v1 whole, which is shorter than its diff:
```python
import functools
import math

import jax
import jax.numpy as jnp
from jax import lax
from jax.experimental import pallas as pl
from jax.experimental.pallas import tpu as pltpu
from jax.sharding import PartitionSpec as P

HD = 128
STEPS = 3
CACHE = 128


EPSILON = 1e-05
NEGATIVE = -1e30
VMEM_LIMIT = 60 * 1024 * 1024
LANES = 128


def ring_spot(index, size):
    side = index % 2
    return index // 2 + side * (size - 1 - 2 * (index // 2))


def ring_index(spot, size):
    spot = (spot + 2 * size) % size
    side = spot // (size // 2)
    return 2 * (spot + side * (size - 1 - 2 * spot)) + side


def swap_pairs(values):
    lanes = values.shape[1]
    even = lax.broadcasted_iota(jnp.int32, values.shape, 1) % 2 == 0
    return jnp.where(even, pltpu.roll(values, lanes - 1, 1), pltpu.roll(values, 1, 1))


def square_lanes(x):
    squares = x * x
    total = squares[:, :LANES]
    for start in range(LANES, x.shape[1], LANES):
        total = total + squares[:, start : start + LANES]
    return total


def input_part(
    size,
    greet,
    small_x,
    base_x,
    small_gain,
    base_gain,
    small_w,
    query_w,
    pair_w,
    lengths,
    small_out,
    query_out,
    pair_out,
    small_box,
    base_box,
    small_tiles,
    query_tiles,
    pair_tiles,
    small_total,
    query_total,
    pair_total,
    small_square,
    base_square,
    small_cos,
    small_sin,
    base_cos,
    base_sin,
    local_sems,
    small_w_sems,
    query_w_sems,
    pair_w_sems,
    small_sends,
    small_receives,
    base_sends,
    base_receives,
    core_sends,
    core_receives,
):
    group = lax.axis_index("grp")
    mine = lax.axis_index("tp")
    data = lax.axis_index("dp")
    turn = 1 - 2 * group
    spot = ring_spot(mine, size)
    ahead = (group, ring_index(spot + turn, size), data)
    behind = (group, ring_index(spot - turn, size), data)
    other_core = (1 - group, mine, data)
    rows, small_width = small_x.shape
    base_width = base_x.shape[1]

    def small_source(step):
        return ring_index(spot - step * turn, size)

    def base_source(side, step):
        index = ring_index(spot - (1 - 2 * side) * step * turn, size)
        return (group + side * (1 - 2 * group)) * size + index

    def small_fetch(step):
        rows = pl.ds(pl.multiple_of(small_source(step) * small_width, small_width), small_width)
        return pltpu.make_async_copy(
            small_w.at[0, :, rows, :], small_tiles.at[step], small_w_sems.at[step]
        )

    def query_fetch(side, step):
        rows = pl.ds(pl.multiple_of(base_source(side, step) * base_width, base_width), base_width)
        return pltpu.make_async_copy(
            query_w.at[rows, :], query_tiles.at[side, step], query_w_sems.at[side, step]
        )

    slice_width = pair_w.shape[1]
    copies = LANES // slice_width

    def pair_fetch(side, step, kind, copy):
        columns = pl.ds(pl.multiple_of(base_source(side, step) * base_width, base_width), base_width)
        return pltpu.make_async_copy(
            pair_w.at[kind, :, columns],
            pair_tiles.at[side, step, pl.ds(kind * LANES + copy * slice_width, slice_width)],
            pair_w_sems.at[side, step, kind * copies + copy],
        )

    def pair_fetches(side, step):
        return [pair_fetch(side, step, kind, copy) for kind in range(2) for copy in range(copies)]

    keeps = [
        pltpu.make_async_copy(small_x, small_box.at[0], local_sems.at[0]),
        pltpu.make_async_copy(base_x, base_box.at[0, 0], local_sems.at[1]),
    ]
    for keep in keeps:
        keep.start()

    def fetch_all(step, carry):
        small_fetch(step).start()
        for side in range(2):
            query_fetch(side, step).start()
            for fetch in pair_fetches(side, step):
                fetch.start()
        return carry

    lax.fori_loop(0, size, fetch_all, 0)
    small_total[...] = jnp.zeros_like(small_total)
    query_total[...] = jnp.zeros_like(query_total)
    pair_total[...] = jnp.zeros_like(pair_total)
    small_square[...] = jnp.zeros_like(small_square)
    base_square[...] = jnp.zeros_like(base_square)
    greet()
    for keep in keeps:
        keep.wait()

    half = size // 2

    def hop(box, source, target, sends, receives, device):
        return pltpu.make_async_remote_copy(
            src_ref=box.at[source],
            dst_ref=box.at[target],
            send_sem=sends.at[target],
            recv_sem=receives.at[target],
            device_id=device,
            device_id_type=pl.DeviceIdType.MESH,
        )

    def small_fore(step):
        return hop(small_box, step, step + 1, small_sends, small_receives, ahead)

    def small_back(step):
        source = (size - step) % size
        return hop(small_box, source, size - step - 1, small_sends, small_receives, behind)

    def base_fore(step):
        return hop(base_box.at[0], step, step + 1, base_sends, base_receives, ahead)

    def base_back(step):
        source = (size - step) % size
        return hop(base_box.at[0], source, size - step - 1, base_sends, base_receives, behind)

    def core_hop(step):
        return pltpu.make_async_remote_copy(
            src_ref=base_box.at[0, step],
            dst_ref=base_box.at[1, step],
            send_sem=core_sends.at[step],
            recv_sem=core_receives.at[step],
            device_id=other_core,
            device_id_type=pl.DeviceIdType.MESH,
        )

    def small_work(step):
        small_fetch(step).wait()
        x = small_box[step].astype(jnp.float32)
        small_square[...] += square_lanes(x)
        scaled = (x * small_gain[small_source(step)]).astype(jnp.bfloat16)
        for part in range(small_tiles.shape[1]):
            small_total[part] += jnp.dot(
                scaled, small_tiles[step, part], preferred_element_type=jnp.float32
            )

    def base_work(side, step):
        query_fetch(side, step).wait()
        for fetch in pair_fetches(side, step):
            fetch.wait()
        x = base_box[side, step].astype(jnp.float32)
        base_square[...] += square_lanes(x)
        scaled = (x * base_gain[base_source(side, step)]).astype(jnp.bfloat16)
        query_total[...] += jnp.dot(
            scaled, query_tiles[side, step], preferred_element_type=jnp.float32
        )
        pair_total[...] += lax.dot_general(
            scaled,
            pair_tiles[side, step],
            (((1,), (1,)), ((), ())),
            preferred_element_type=jnp.float32,
        )

    small_fore(0).start()
    small_back(0).start()
    base_fore(0).start()
    base_back(0).start()
    core_hop(0).start()

    def place(row, carry):
        small_cos[pl.ds(row, 1), :] = jnp.full((1, LANES), lengths[row].astype(jnp.float32))
        return carry

    row_count = rows // STEPS
    lax.fori_loop(0, row_count, place, 0)
    start = small_cos[:row_count, :]
    lane = lax.broadcasted_iota(jnp.int32, (1, LANES), 1)
    sign = jnp.where(lane % 2 == 0, -1.0, 1.0)

    def fill_tables(cosine, sine, first_pair, width):
        pair_index = (first_pair + (lane % width) // 2).astype(jnp.float32)
        frequency = jnp.exp(pair_index * (-2.0 * math.log(10000.0) / HD))
        for step in range(STEPS):
            angles = (start + float(step)) * frequency
            piece = slice(step * row_count, (step + 1) * row_count)
            cosine[piece, :] = jnp.cos(angles)
            sine[piece, :] = jnp.sin(angles) * sign

    fill_tables(base_cos, base_sin, mine % copies * (slice_width // 2), slice_width)
    fill_tables(small_cos, small_sin, 0, HD)
    small_work(0)
    base_work(0, 0)

    def ring_step(step, carry):
        small_fore(step - 1).wait_recv()
        small_fore(step).start()
        small_back(step - 1).wait_recv()

        @pl.when(step < half - 1)
        def _():
            small_back(step).start()

        small_work(step)
        small_work(size - step)
        base_fore(step - 1).wait_recv()
        base_fore(step).start()
        base_back(step - 1).wait_recv()

        @pl.when(step < half - 1)
        def _():
            base_back(step).start()

        core_hop(step).start()
        core_hop(size - step).start()
        base_work(0, step)
        base_work(0, size - step)
        core_hop(step - 1).wait_recv()
        base_work(1, step - 1)

        @pl.when(step > 1)
        def _():
            core_hop(size + 1 - step).wait_recv()
            base_work(1, size + 1 - step)

        return carry

    lax.fori_loop(1, half, ring_step, 0)
    core_hop(half - 1).wait_recv()
    base_work(1, half - 1)
    if half > 1:
        core_hop(half + 1).wait_recv()
        base_work(1, half + 1)
    small_fore(half - 1).wait_recv()
    small_work(half)
    base_fore(half - 1).wait_recv()
    core_hop(half).start()
    base_work(0, half)
    core_hop(half).wait_recv()
    base_work(1, half)

    def settle(step, carry):
        small_fore(step).wait_send()
        base_fore(step).wait_send()
        return carry

    def settle_back(step, carry):
        small_back(step).wait_send()
        base_back(step).wait_send()
        return carry

    def settle_core(step, carry):
        core_hop(step).wait_send()
        return carry

    lax.fori_loop(0, half, settle, 0)
    lax.fori_loop(0, half - 1, settle_back, 0)
    lax.fori_loop(0, size, settle_core, 0)

    def scale_of(square_ref, width):
        total = jnp.sum(square_ref[...], axis=-1, keepdims=True)
        return lax.rsqrt(total / width + EPSILON)

    def store(ref, index, values):
        ref[index + (slice(0, rows),)] = values.astype(jnp.bfloat16).astype(jnp.float32)
        rest = ref.shape[-2] - rows
        ref[index + (slice(rows, rows + rest),)] = jnp.zeros((rest, LANES), jnp.float32)

    scale = scale_of(small_square, size * small_width)
    for part in range(small_out.shape[0]):
        for tile in range(small_out.shape[1]):
            columns = slice(tile * LANES, (tile + 1) * LANES)
            values = small_total[part, :, columns] * scale
            if part < 2:
                values = values * small_cos[...] + swap_pairs(values) * small_sin[...]
            store(small_out, (part, tile), values)
    scale = scale_of(base_square, 2 * size * base_width)
    for tile in range(query_out.shape[0]):
        columns = slice(tile * LANES, (tile + 1) * LANES)
        values = query_total[:, columns] * scale
        values = values * base_cos[...] + swap_pairs(values) * base_sin[...]
        store(query_out, (tile,), values)
    values = pair_total[:, :LANES] * scale
    values = values * base_cos[...] + swap_pairs(values) * base_sin[...]
    store(pair_out, (0,), values)
    store(pair_out, (1,), pair_total[:, LANES:] * scale)


def attention_part(
    share,
    begin,
    between,
    small_qkv,
    query,
    pair,
    lengths,
    small_cache,
    base_cache,
    small_out,
    base_out,
    small_keys,
    small_values,
    base_keys,
    base_values,
    small_scores,
    small_fresh,
    small_weights,
    small_fresh_weights,
    base_scores,
    base_stage,
    base_land,
    small_result,
    base_result,
    small_sems,
    base_sems,
    share_sends,
    share_receives,
):
    group = lax.axis_index("grp")
    mine = lax.axis_index("tp")
    data = lax.axis_index("dp")
    row_count = small_keys.shape[0]
    chunk = row_count // small_sems.shape[1]
    chunks = small_sems.shape[1]
    part_rows = small_scores.shape[1]
    base_rows = base_scores.shape[1]
    slice_width = base_cache.shape[2]
    copies = LANES // slice_width
    factor = 1.0 / math.sqrt(HD)
    near = mine - mine % share

    def peer(step):
        return (group, near + (mine % share + step) % share, data)

    def small_fetch(kind, index):
        rows = pl.ds(index * chunk, chunk)
        target = (small_keys, small_values)[kind]
        return pltpu.make_async_copy(
            small_cache.at[0, kind, rows], target.at[rows], small_sems.at[kind, index]
        )

    def base_fetch(kind, copy):
        target = (base_keys, base_values)[kind]
        return pltpu.make_async_copy(
            base_cache.at[kind],
            target.at[:, pl.ds(copy * slice_width, slice_width)],
            base_sems.at[kind, copy],
        )

    for copy in range(copies):
        base_fetch(0, copy).start()
    for kind in range(2):

        def fetch(index, carry, kind=kind):
            small_fetch(kind, index).start()
            return carry

        lax.fori_loop(0, chunks, fetch, 0)
    for copy in range(copies):
        base_fetch(1, copy).start()
    begin()

    def four(ref, row):
        return ref[pl.ds(row, 4, stride=row_count), :]

    def share_copy(step, index):
        rows = pl.ds(index * chunk, chunk)
        return pltpu.make_async_remote_copy(
            src_ref=base_stage.at[rows],
            dst_ref=base_land.at[step - 1, rows],
            send_sem=share_sends.at[step - 1, index],
            recv_sem=share_receives.at[step - 1, index],
            device_id=peer(step),
            device_id_type=pl.DeviceIdType.MESH,
        )

    def nt(x, y):
        return lax.dot_general(x, y, (((1,), (1,)), ((), ())), preferred_element_type=jnp.float32)

    wide = (base_rows, LANES)
    row = lax.broadcasted_iota(jnp.int32, wide, 0)
    lane = lax.broadcasted_iota(jnp.int32, wide, 1)
    base_mask = lane // slice_width == (row // 4) % copies
    step_of = row % 4
    fresh_lanes = [lane // 8 == step_of + odd * (LANES // 16) for odd in range(2)]
    fresh_masks = [
        lanes & (lane % 8 <= step_of) & (lane % 8 < STEPS) for lanes in fresh_lanes
    ]

    for copy in range(copies):
        base_fetch(0, copy).wait()

    def base_left(r):
        tiles = [four(query.at[g // copies], r) for g in range(base_rows // 4)]
        return jnp.where(base_mask, jnp.concatenate(tiles, axis=0), 0.0).astype(jnp.bfloat16)

    def fresh_rows(ref, r):
        both = [[four(ref, r + odd)] * (LANES // 8) for odd in range(2)]
        return jnp.concatenate(both[0] + both[1], axis=0).astype(jnp.bfloat16)

    def base_score(index, carry):
        for inner in range(0, chunk, 2):
            r = index * chunk + inner
            left = jnp.concatenate([base_left(r), base_left(r + 1)], axis=0)
            keys = jnp.concatenate([base_keys[r], base_keys[r + 1]], axis=1)
            both = jnp.dot(left, keys, preferred_element_type=jnp.float32)
            fresh_both = nt(left, fresh_rows(pair.at[0], r))
            for odd in range(2):
                rows = slice(odd * base_rows, (odd + 1) * base_rows)
                scores = both[rows, odd * LANES : (odd + 1) * LANES]
                fresh = jnp.where(fresh_lanes[odd], fresh_both[rows], 0.0)
                moved = pltpu.roll(fresh, 1, 0) + pltpu.roll(fresh, 2, 0) + pltpu.roll(fresh, 3, 0)
                scores = jnp.where(step_of == 3, moved, scores)
                base_scores[r + odd] = scores
                base_stage[r + odd] = scores.astype(base_stage.dtype)
        for step in range(1, share):
            share_copy(step, index).start()
        return carry

    lax.fori_loop(0, chunks, base_score, 0)

    depth = small_keys.shape[1]
    small_row = lax.broadcasted_iota(jnp.int32, (part_rows, depth), 0)
    small_lane = lax.broadcasted_iota(jnp.int32, (part_rows, depth), 1)
    small_mask = small_lane // HD == small_row // 4
    cached_lane = lax.broadcasted_iota(jnp.int32, (part_rows, LANES), 1)
    fresh_step = lax.broadcasted_iota(jnp.int32, (part_rows, 8), 0) % 4
    fresh_index = lax.broadcasted_iota(jnp.int32, (part_rows, 8), 1)
    small_fresh_masks = [
        (fresh_index >= 4 * odd) & (fresh_index <= 4 * odd + fresh_step) & (fresh_index < 4 * odd + STEPS)
        for odd in range(2)
    ]

    def heads_of(part, row, times):
        heads = [four(small_qkv.at[part, head], row) for head in range(depth // HD)]
        heads = [jnp.concatenate([head] * times, axis=0) for head in heads]
        return jnp.concatenate(heads, axis=1)

    def small_left(r):
        left = jnp.where(small_mask, heads_of(0, r, part_rows // 4), 0.0)
        return left.astype(jnp.bfloat16)

    def small_score(index, carry):
        small_fetch(0, index).wait()
        for inner in range(0, chunk, 2):
            r = index * chunk + inner
            left = jnp.concatenate([small_left(r), small_left(r + 1)], axis=0)
            keys = jnp.concatenate([small_keys[r], small_keys[r + 1]], axis=1)
            both = jnp.dot(left, keys, preferred_element_type=jnp.float32)
            fresh_keys = jnp.concatenate([heads_of(1, r, 1), heads_of(1, r + 1, 1)], axis=0)
            fresh = nt(left, fresh_keys.astype(jnp.bfloat16))
            for odd in range(2):
                rows = slice(odd * part_rows, (odd + 1) * part_rows)
                small_scores[r + odd] = both[rows, odd * CACHE : (odd + 1) * CACHE]
                small_fresh[r + odd] = fresh[rows]
        return carry

    lax.fori_loop(0, chunks, small_score, 0)

    def small_softmax(index, carry):
        for inner in range(chunk):
            r = index * chunk + inner
            cached = jnp.where(cached_lane < lengths[r], small_scores[r] * factor, NEGATIVE)
            fresh = jnp.where(small_fresh_masks[inner % 2], small_fresh[r] * factor, NEGATIVE)
            row_max = jnp.maximum(
                jnp.max(cached, axis=-1, keepdims=True), jnp.max(fresh, axis=-1, keepdims=True)
            )
            cached = jnp.exp(cached - row_max)
            fresh = jnp.exp(fresh - row_max)
            total = jnp.sum(cached, axis=-1, keepdims=True) + jnp.sum(
                fresh, axis=-1, keepdims=True
            )
            small_weights[r] = (cached / total).astype(jnp.bfloat16)
            small_fresh_weights[r] = (fresh / total).astype(jnp.bfloat16).astype(jnp.float32)
        return carry

    lax.fori_loop(0, chunks, small_softmax, 0)

    def small_value(index, carry):
        small_fetch(1, index).wait()
        for inner in range(0, chunk, 2):
            r = index * chunk + inner
            none = jnp.zeros((part_rows, CACHE), jnp.bfloat16)
            first = jnp.concatenate([small_weights[r], none], axis=1)
            second = jnp.concatenate([none, small_weights[r + 1]], axis=1)
            left = jnp.concatenate([first, second], axis=0)
            values = jnp.concatenate([small_values[r], small_values[r + 1]], axis=1)
            both = nt(left, values)
            for odd in range(2):
                fresh_values = heads_of(2, r + odd, 1)
                weights = small_fresh_weights[r + odd]
                for head in range(depth // HD):
                    columns = slice(head * HD, (head + 1) * HD)
                    rows = slice(4 * head, 4 * head + 4)
                    total = both[odd * part_rows + 4 * head : odd * part_rows + 4 * head + 4, columns]
                    for n in range(STEPS):
                        total = total + (
                            weights[rows, 4 * odd + n : 4 * odd + n + 1]
                            * fresh_values[n : n + 1, columns]
                        )
                    small_result[head, pl.ds(r + odd, 4, stride=row_count), :] = total
        return carry

    lax.fori_loop(0, chunks, small_value, 0)
    rows = small_out.shape[0]
    for head in range(depth // HD):
        small_out[:, head * HD : (head + 1) * HD] = small_result[head, :rows].astype(small_out.dtype)

    between()
    for copy in range(copies):
        base_fetch(1, copy).wait()

    def base_softmax(r, odd):
        scores = base_scores[r]
        for step in range(share - 1):
            scores = scores + base_land[step, r].astype(jnp.float32)
        fresh = jnp.where(
            step_of == 0,
            pltpu.roll(scores, base_rows - 3, 0),
            jnp.where(
                step_of == 1,
                pltpu.roll(scores, base_rows - 2, 0),
                pltpu.roll(scores, base_rows - 1, 0),
            ),
        )
        cached = jnp.where(lane < lengths[r], scores * factor, NEGATIVE)
        fresh = jnp.where(fresh_masks[odd], fresh * factor, NEGATIVE)
        row_max = jnp.max(jnp.maximum(cached, fresh), axis=-1, keepdims=True)
        cached = jnp.exp(cached - row_max)
        fresh = jnp.exp(fresh - row_max)
        total = jnp.sum(cached + fresh, axis=-1, keepdims=True)
        return (cached / total).astype(jnp.bfloat16), (fresh / total).astype(jnp.bfloat16)

    def base_value(index, carry):
        for step in range(1, share):
            share_copy(step, index).wait_recv()
        for inner in range(0, chunk, 2):
            r = index * chunk + inner
            none = jnp.zeros((base_rows, CACHE), jnp.bfloat16)
            cached, fresh = zip(base_softmax(r, 0), base_softmax(r + 1, 1))
            first = jnp.concatenate([cached[0], none], axis=1)
            second = jnp.concatenate([none, cached[1]], axis=1)
            left = jnp.concatenate([first, second], axis=0)
            values = jnp.concatenate([base_values[r], base_values[r + 1]], axis=1)
            both = nt(left, values) + jnp.dot(
                jnp.concatenate(fresh, axis=0),
                fresh_rows(pair.at[1], r),
                preferred_element_type=jnp.float32,
            )
            for odd in range(2):
                heads = both[odd * base_rows : (odd + 1) * base_rows]
                for tile in range(base_out.shape[1] // LANES):
                    g = tile * copies
                    part = heads[4 * g : 4 * g + 4]
                    for copy in range(1, copies):
                        g = tile * copies + copy
                        part = jnp.where(
                            lane[:4] // slice_width == copy, heads[4 * g : 4 * g + 4], part
                        )
                    base_result[tile, pl.ds(r + odd, 4, stride=row_count), :] = part
        return carry

    lax.fori_loop(0, chunks, base_value, 0)
    for tile in range(base_out.shape[1] // LANES):
        base_out[:, tile * LANES : (tile + 1) * LANES] = base_result[tile, :rows].astype(
            base_out.dtype
        )

    def settle(index, carry):
        for step in range(1, share):
            share_copy(step, index).wait_send()
        return carry

    lax.fori_loop(0, chunks, settle, 0)


def output_part(
    size,
    small_heads,
    base_heads,
    small_gain,
    base_gain,
    next_tokens,
    small_w,
    base_w,
    small_table,
    base_table,
    log_out,
    norm_out,
    chosen_out,
    small_w_tiles,
    base_w_tiles,
    small_stage,
    small_land,
    base_stage,
    base_land,
    core_stage,
    core_land,
    small_box,
    base_box,
    small_logits,
    base_logits,
    theirs,
    small_square,
    base_square,
    stats,
    stats_box,
    tokens,
    small_w_sems,
    base_w_sems,
    small_t_sems,
    base_t_sems,
    sum_sends,
    sum_receives,
    swap_sends,
    swap_receives,
    ring_sends,
    ring_receives,
    core_sends,
    core_receives,
    gap_sems,
    stat_sends,
    stat_receives,
):
    group = lax.axis_index("grp")
    mine = lax.axis_index("tp")
    data = lax.axis_index("dp")
    turn = 1 - 2 * group
    spot = ring_spot(mine, size)
    ahead = (group, ring_index(spot + turn, size), data)
    behind = (group, ring_index(spot - turn, size), data)
    other_core = (1 - group, mine, data)
    place = group * size + mine
    count = 2 * size
    rows, small_width = small_box.shape[1:]
    base_width = base_box.shape[3]
    width = base_table.shape[0]
    row_count = rows // STEPS

    def peer(step):
        index = (place + step) % count
        return (index // size, index % size, data)

    def small_source(step):
        return ring_index(spot - step * turn, size)

    def base_source(side, step):
        index = ring_index(spot - (1 - 2 * side) * step * turn, size)
        return (group + side * (1 - 2 * group)) * size + index

    def columns(block, width):
        return pl.ds(pl.multiple_of(block * width, width), width)

    half = size // 2

    def slot_of(use):
        odd = use % 2
        return odd * ((use + 1) // 2) + (1 - odd) * ((size - use // 2) % size)

    def small_w_fetch(tile):
        return pltpu.make_async_copy(
            small_w.at[0, :, columns(small_source(tile), small_width)],
            small_w_tiles.at[tile],
            small_w_sems.at[tile],
        )

    def base_w_fetch(side, tile):
        return pltpu.make_async_copy(
            base_w.at[:, columns(base_source(side, tile), base_width)],
            base_w_tiles.at[side, tile],
            base_w_sems.at[side, tile],
        )

    def remote(source, target, sends, receives, device):
        return pltpu.make_async_remote_copy(
            src_ref=source,
            dst_ref=target,
            send_sem=sends,
            recv_sem=receives,
            device_id=device,
            device_id_type=pl.DeviceIdType.MESH,
        )

    def sum_hop(model, tile, device):
        stage, land = ((small_stage, small_land), (base_stage, base_land))[model]
        return remote(
            stage.at[tile], land.at[tile], sum_sends.at[model, tile], sum_receives.at[model, tile], device
        )

    def sum_fore(model, step):
        return sum_hop(model, half + step, ahead)

    def sum_back(model, step):
        return sum_hop(model, half - 1 - step, behind)

    def core_sum(tile):
        return remote(
            core_stage.at[tile],
            core_land.at[tile],
            swap_sends.at[tile],
            swap_receives.at[tile],
            other_core,
        )

    def hop(model, source, target, device):
        box = small_box if model == 0 else base_box.at[0]
        return remote(
            box.at[source],
            box.at[target],
            ring_sends.at[model, target],
            ring_receives.at[model, target],
            device,
        )

    def fore(model, step):
        return hop(model, step, step + 1, ahead)

    def back(model, step):
        return hop(model, (size - step) % size, size - step - 1, behind)

    def core_hop(step):
        return remote(
            base_box.at[0, step],
            base_box.at[1, step],
            core_sends.at[step],
            core_receives.at[step],
            other_core,
        )

    def begin():
        def fetch_w(step, carry):
            small_w_fetch(half + step).start()
            small_w_fetch(half - 1 - step).start()
            return carry

        def fetch_base_w(step, carry):
            base_w_fetch(1, half + step).start()
            base_w_fetch(0, half + step).start()
            base_w_fetch(1, half - 1 - step).start()
            base_w_fetch(0, half - 1 - step).start()
            return carry

        lax.fori_loop(0, half, fetch_w, 0)
        lax.fori_loop(0, half, fetch_base_w, 0)
        small_logits[...] = jnp.zeros_like(small_logits)
        base_logits[...] = jnp.zeros_like(base_logits)
        small_square[...] = jnp.zeros_like(small_square)
        base_square[...] = jnp.zeros_like(base_square)

    def small_part(tile):
        small_w_fetch(tile).wait()
        return jnp.dot(small_heads[...], small_w_tiles[tile], preferred_element_type=jnp.float32)

    def base_part(side, tile):
        base_w_fetch(side, tile).wait()
        return jnp.dot(
            base_heads[...], base_w_tiles[side, tile], preferred_element_type=jnp.float32
        )

    def core_send(tile):
        core_stage[tile] = base_part(1, tile).astype(core_stage.dtype)
        core_sum(tile).start()

    def small_send(tile, device, before):
        total = small_part(tile)
        if before is not None:
            sum_hop(0, before, device).wait_recv()
            total = total + small_land[before].astype(jnp.float32)
        small_stage[tile] = total.astype(small_stage.dtype)
        sum_hop(0, tile, device).start()

    def base_send(tile, device, before):
        total = base_part(0, tile)
        core_sum(tile).wait_recv()
        total = total + core_land[tile].astype(jnp.float32)
        if before is not None:
            sum_hop(1, before, device).wait_recv()
            total = total + base_land[before].astype(jnp.float32)
        base_stage[tile] = total.astype(base_stage.dtype)
        sum_hop(1, tile, device).start()

    def start_small():
        small_send(half, ahead, None)
        if half > 1:
            small_send(half - 1, behind, None)

    def rest(small_tiles, base_tiles):
        slots = small_tiles.shape[0]

        def small_fetch(use):
            return pltpu.make_async_copy(
                small_table.at[0, :, :, columns(small_source(slot_of(use)), small_width)],
                small_tiles.at[use % slots],
                small_t_sems.at[use],
            )

        def base_fetch(side, use):
            return pltpu.make_async_copy(
                base_table.at[:, columns(base_source(side, slot_of(use)), base_width)],
                base_tiles.at[side, use % slots],
                base_t_sems.at[side, use],
            )

        for step in range(min(slots, size)):
            small_fetch(step).start()
            base_fetch(0, step).start()
            base_fetch(1, step).start()
        core_send(half)
        if half > 1:
            core_send(half - 1)
        base_send(half, ahead, None)
        if half > 1:
            base_send(half - 1, behind, None)
            core_send(half + 1)
            core_send(half - 2)

        def sum_step(step, carry):
            small_send(half + step, ahead, half + step - 1)
            small_send(half - 1 - step, behind, half - step)
            core_send(half + step + 1)
            core_send(half - 2 - step)
            base_send(half + step, ahead, half + step - 1)
            base_send(half - 1 - step, behind, half - step)
            return carry

        lax.fori_loop(1, half - 1, sum_step, 0)
        last = size - 1
        if half > 1:
            small_send(last, ahead, last - 1)
        total = small_part(0) + small_box[0].astype(jnp.float32)
        if half > 1:
            base_send(last, ahead, last - 1)
        else:
            core_send(0)
        if half > 1:
            sum_hop(0, 1, behind).wait_recv()
            total = total + small_land[1].astype(jnp.float32)
        sum_hop(0, last, ahead).wait_recv()
        total = total + small_land[last].astype(jnp.float32)
        small_box[0] = total.astype(small_box.dtype)
        fore(0, 0).start()
        if half > 1:
            back(0, 0).start()
        total = base_part(0, 0) + base_box[0, 0].astype(jnp.float32)
        core_sum(0).wait_recv()
        total = total + core_land[0].astype(jnp.float32)
        if half > 1:
            sum_hop(1, 1, behind).wait_recv()
            total = total + base_land[1].astype(jnp.float32)
        sum_hop(1, last, ahead).wait_recv()
        total = total + base_land[last].astype(jnp.float32)
        base_box[0, 0] = total.astype(base_box.dtype)
        fore(1, 0).start()
        if half > 1:
            back(1, 0).start()
        core_hop(0).start()

        def place_tokens(row, carry):
            for step in range(STEPS):
                token = next_tokens[step, row] - place * width
                tokens[pl.ds(step * row_count + row, 1), :] = jnp.full((1, LANES), token, jnp.int32)
            return carry

        lax.fori_loop(0, row_count, place_tokens, 0)

        def times(x, table):
            return lax.dot_general(
                x, table, (((1,), (1,)), ((), ())), preferred_element_type=jnp.float32
            )

        def small_work(use):
            small_fetch(use).wait()
            slot = slot_of(use)
            x = small_box[slot].astype(jnp.float32)
            small_square[...] += square_lanes(x)
            scaled = (x * small_gain[small_source(slot)]).astype(jnp.bfloat16)
            for part in range(2):
                small_logits[part] += times(scaled, small_tiles[use % slots, part])

            @pl.when(use + slots < size)
            def _():
                small_fetch(use + slots).start()

        def base_work(side, use):
            base_fetch(side, use).wait()
            slot = slot_of(use)
            x = base_box[side, slot].astype(jnp.float32)
            base_square[...] += square_lanes(x)
            scaled = (x * base_gain[base_source(side, slot)]).astype(jnp.bfloat16)
            base_logits[...] += times(scaled, base_tiles[side, use % slots])

            @pl.when(use + slots < size)
            def _():
                base_fetch(side, use + slots).start()

        small_work(0)
        base_work(0, 0)
        core_hop(0).wait_recv()
        base_work(1, 0)

        def ring_step(step, carry):
            fore(0, step - 1).wait_recv()
            fore(0, step).start()
            back(0, step - 1).wait_recv()

            @pl.when(step < half - 1)
            def _():
                back(0, step).start()

            small_work(2 * step - 1)
            small_work(2 * step)
            fore(1, step - 1).wait_recv()
            fore(1, step).start()
            back(1, step - 1).wait_recv()

            @pl.when(step < half - 1)
            def _():
                back(1, step).start()

            core_hop(step).start()
            core_hop(size - step).start()
            base_work(0, 2 * step - 1)
            base_work(0, 2 * step)
            core_hop(step).wait_recv()
            base_work(1, 2 * step - 1)
            core_hop(size - step).wait_recv()
            base_work(1, 2 * step)
            return carry

        lax.fori_loop(1, half, ring_step, 0)
        fore(0, half - 1).wait_recv()
        small_work(size - 1)

        def scale_of(square_ref, width):
            total = jnp.sum(square_ref[...], axis=-1, keepdims=True)
            return lax.rsqrt(total / width + EPSILON)

        scale = scale_of(small_square, size * small_width)
        for part in range(2):
            small_logits[part] = small_logits[part] * scale
        gap = remote(
            small_logits.at[1 - group], theirs, gap_sems.at[0], gap_sems.at[1], other_core
        )
        gap.start()
        fore(1, half - 1).wait_recv()
        core_hop(half).start()
        base_work(0, size - 1)
        core_hop(half).wait_recv()
        base_work(1, size - 1)
        scale = scale_of(base_square, count * base_width)
        gap.wait_recv()
        sign = turn.astype(jnp.float32)
        steered = base_logits[...] * scale + sign * (small_logits[group] - theirs[...])
        log_out[...] = steered
        row_max = jnp.max(steered, axis=-1, keepdims=True)
        exp_total = jnp.sum(jnp.exp(steered - row_max), axis=-1, keepdims=True)
        lane = lax.broadcasted_iota(jnp.int32, (rows, LANES), 1)
        picked = jnp.zeros((rows, LANES), jnp.float32)
        for start in range(0, width, LANES):
            hit = lane + start == tokens[...]
            picked = picked + jnp.where(hit, log_out[:, start : start + LANES], 0.0)
        picked = jnp.sum(picked, axis=-1, keepdims=True)
        packed = jnp.where(lane == 0, row_max, jnp.where(lane == 1, exp_total, picked))
        stats[...] = jnp.zeros_like(stats)
        stats[:rows] = packed
        turned = stats[...].T
        stats_box[place] = turned[:8]

        def share(step):
            return remote(
                stats_box.at[place],
                stats_box.at[place],
                stat_sends.at[step],
                stat_receives.at[step],
                peer(step),
            )

        def share_start(step, carry):
            share(step).start()
            return carry

        def share_wait(step, carry):
            share(step).wait_recv()
            return carry

        lax.fori_loop(1, count, share_start, 0)
        lax.fori_loop(1, count, share_wait, 0)
        everyone = stats_box[...]
        maxima = everyone[:, 0:1]
        row_max = jnp.max(maxima, axis=0)
        exp_total = jnp.sum(everyone[:, 1:2] * jnp.exp(maxima - row_max[None]), axis=0)
        log_norm = row_max + jnp.log(exp_total)
        chosen = jnp.sum(everyone[:, 2:3], axis=0) - log_norm
        pick = lax.broadcasted_iota(jnp.int32, (LANES, log_norm.shape[1]), 0)
        columns_out = jnp.where(pick == 0, log_norm, chosen).T
        norm_out[...] = columns_out[:rows]
        chosen = columns_out[:row_count]
        for step in range(1, STEPS):
            chosen = chosen + columns_out[step * row_count : (step + 1) * row_count]
        chosen_out[...] = chosen

        def settle(step, carry):
            for model in range(2):
                sum_fore(model, step).wait_send()
                fore(model, step).wait_send()
            return carry

        def settle_back(step, carry):
            for model in range(2):
                sum_back(model, step).wait_send()
                back(model, step).wait_send()
            return carry

        def settle_core(step, carry):
            core_sum(step).wait_send()
            core_hop(step).wait_send()
            return carry

        lax.fori_loop(0, half, settle, 0)
        lax.fori_loop(0, half - 1, settle_back, 0)
        lax.fori_loop(0, size, settle_core, 0)
        gap.wait_send()

        def share_settle(step, carry):
            share(step).wait_send()
            return carry

        lax.fori_loop(1, count, share_settle, 0)

    return begin, start_small, rest


def whole_kernel(
    size,
    share,
    slots,
    small_x,
    base_x,
    small_gain,
    base_gain,
    small_final,
    base_final,
    lengths,
    next_tokens,
    small_w,
    query_w,
    pair_w,
    small_cache,
    base_cache,
    small_out_w,
    base_out_w,
    small_table,
    base_table,
    steered,
    norm,
    chosen,
    small_box,
    base_box,
    small_qkv,
    query,
    pair,
    small_square,
    base_square,
    small_heads,
    base_heads,
    input_sems,
    attention_scratch,
    attention_sems,
    output_scratch,
    output_sems,
):
    group = lax.axis_index("grp")
    mine = lax.axis_index("tp")
    data = lax.axis_index("dp")
    place = group * size + mine
    count = 2 * size
    rows, small_width = small_box.shape[1:]
    base_width = base_box.shape[3]
    row_count, depth = small_cache.shape[2:4]
    parts = small_w.shape[1]
    half = jnp.bfloat16

    def greet():
        barrier = pltpu.get_barrier_semaphore()

        def call(step, carry):
            index = (place + step) % count
            pl.semaphore_signal(
                barrier,
                inc=1,
                device_id=(index // size, index % size, data),
                device_id_type=pl.DeviceIdType.MESH,
            )
            return carry

        lax.fori_loop(1, count, call, 0)
        pl.semaphore_wait(barrier, count - 1)

    def first(small_tiles, query_tiles, pair_tiles, small_total, query_total, pair_total, *tables):
        input_part(
            size,
            greet,
            small_x,
            base_x,
            small_gain,
            base_gain,
            small_w,
            query_w,
            pair_w,
            lengths,
            small_qkv,
            query,
            pair,
            small_box,
            base_box,
            small_tiles,
            query_tiles,
            pair_tiles,
            small_total,
            query_total,
            pair_total,
            small_square,
            base_square,
            *tables,
            *input_sems,
        )

    table = pltpu.VMEM((rows, LANES), jnp.float32)
    pl.run_scoped(
        first,
        pltpu.VMEM((size, parts, small_width, depth), half),
        pltpu.VMEM((2, size, base_width, query_w.shape[1]), half),
        pltpu.VMEM((2, size, 2 * LANES, base_width), half),
        pltpu.VMEM((parts, rows, depth), jnp.float32),
        pltpu.VMEM((rows, query_w.shape[1]), jnp.float32),
        pltpu.VMEM((rows, 2 * LANES), jnp.float32),
        table,
        table,
        table,
        table,
    )
    def after(small_w_tiles, base_w_tiles):
        begin, start_small, rest = output_part(
            size,
            small_heads,
            base_heads,
            small_final,
            base_final,
            next_tokens,
            small_out_w,
            base_out_w,
            small_table,
            base_table,
            steered,
            norm,
            chosen,
            small_w_tiles,
            base_w_tiles,
            *output_scratch[:6],
            small_box,
            base_box,
            *output_scratch[6:9],
            small_square,
            base_square,
            *output_scratch[9:],
            *output_sems,
        )

        def between():
            start_small()

        def second(small_keys, small_values, base_keys, base_values):
            attention_part(
                share,
                begin,
                between,
                small_qkv,
                query,
                pair,
                lengths,
                small_cache,
                base_cache,
                small_heads,
                base_heads,
                small_keys,
                small_values,
                base_keys,
                base_values,
                *attention_scratch,
                *attention_sems,
            )

        cache = pltpu.VMEM((row_count, depth, CACHE), half)
        wide = pltpu.VMEM((row_count, LANES, CACHE), half)
        pl.run_scoped(second, cache, cache, wide, wide)
        vocab = base_table.shape[0]
        pl.run_scoped(
            rest,
            pltpu.VMEM((slots, 2, vocab, small_width), half),
            pltpu.VMEM((2, slots, vocab, base_width), half),
        )

    output_depth = base_out_w.shape[0]
    pl.run_scoped(
        after,
        pltpu.VMEM((size, depth, small_width), half),
        pltpu.VMEM((2, size, output_depth, base_width), half),
    )


def whole_stage(
    small_x,
    base_x,
    small_gain,
    base_gain,
    small_final,
    base_final,
    lengths,
    next_tokens,
    small_w,
    query_w,
    pair_w,
    small_cache,
    base_cache,
    small_out_w,
    base_out_w,
    small_table,
    base_table,
):
    size = lax.axis_size("tp")
    rows, small_width = small_x.shape
    base_width = base_x.shape[1]
    row_count, depth = small_cache.shape[2:4]
    base_depth = query_w.shape[1]
    slice_width = base_cache.shape[2]
    share = HD // slice_width
    copies = LANES // slice_width
    base_rows = 4 * (base_depth // slice_width)
    part_rows = max(8, 4 * (depth // HD))
    chunks = row_count // 8
    parts = small_w.shape[1]
    padded = rows // STEPS * (STEPS + 1)
    vocab = base_table.shape[0]
    stat_rows = rows + -rows % LANES
    slots = 3
    half = jnp.bfloat16
    wide = jnp.float32
    vmem = pl.BlockSpec(memory_space=pltpu.VMEM)
    smem = pl.BlockSpec(memory_space=pltpu.SMEM)
    hbm = pl.BlockSpec(memory_space=pl.ANY)
    dma = pltpu.SemaphoreType.DMA
    space = pltpu.VMEM
    return pl.pallas_call(
        functools.partial(whole_kernel, size, share, slots),
        in_specs=[hbm] * 2 + [vmem] * 4 + [smem] * 2 + [hbm] * 9,
        out_specs=[vmem] * 3,
        out_shape=[
            jax.ShapeDtypeStruct((rows, vocab), wide),
            jax.ShapeDtypeStruct((rows, LANES), wide),
            jax.ShapeDtypeStruct((row_count, LANES), wide),
        ],
        scratch_shapes=[
            space((size, rows, small_width), half),
            space((2, size, rows, base_width), half),
            space((parts, depth // LANES, padded, LANES), wide),
            space((base_depth // LANES, padded, LANES), wide),
            space((2, padded, LANES), wide),
            space((rows, LANES), wide),
            space((rows, LANES), wide),
            space((rows, depth), half),
            space((rows, base_depth), half),
            [dma((2,)), dma((size,)), dma((2, size)), dma((2, size, 2 * copies))]
            + [dma((size,))] * 6,
            [
                space((row_count, part_rows, CACHE), wide),
                space((row_count, part_rows, 8), wide),
                space((row_count, part_rows, CACHE), half),
                space((row_count, part_rows, 8), wide),
                space((row_count, base_rows, CACHE), wide),
                space((row_count, base_rows, CACHE), half),
                space((share - 1, row_count, base_rows, CACHE), half),
                space((depth // LANES, padded, LANES), wide),
                space((base_depth // LANES, padded, LANES), wide),
            ],
            [dma((2, chunks)), dma((2, copies)), dma((share - 1, chunks)), dma((share - 1, chunks))],
            [space((size, rows, small_width), half)] * 2
            + [space((size, rows, base_width), half)] * 4
            + [
                space((2, rows, vocab), wide),
                space((rows, vocab), wide),
                space((rows, vocab), wide),
                space((stat_rows, LANES), wide),
                space((2 * size, 8, stat_rows), wide),
                space((rows, LANES), jnp.int32),
            ],
            [
                dma((size,)),
                dma((2, size)),
                dma((size,)),
                dma((2, size)),
                dma((2, size)),
                dma((2, size)),
                dma((size,)),
                dma((size,)),
                dma((2, size)),
                dma((2, size)),
                dma((size,)),
                dma((size,)),
                dma((2,)),
                dma((2 * size,)),
                dma((2 * size,)),
            ],
        ],
        compiler_params=pltpu.CompilerParams(
            collective_id=0, has_side_effects=True, vmem_limit_bytes=VMEM_LIMIT
        ),
    )(
        small_x,
        base_x,
        small_gain.reshape(size, 1, small_width),
        base_gain.reshape(2 * size, 1, base_width),
        small_final.reshape(size, 1, small_width),
        base_final.reshape(2 * size, 1, base_width),
        lengths,
        next_tokens,
        small_w,
        query_w,
        pair_w,
        small_cache,
        base_cache,
        small_out_w,
        base_out_w,
        small_table,
        base_table,
    )


def finish_kernel(steered, norm, chosen, log_out, chosen_out):
    log_out[...] = steered[...] - norm[:, :1]
    chosen_out[...] = chosen[...].T[1:2]


def finish(steered, norm, chosen):
    whole = pl.BlockSpec(memory_space=pltpu.VMEM)
    return pl.pallas_call(
        finish_kernel,
        in_specs=[whole] * 3,
        out_specs=[whole] * 2,
        out_shape=[
            jax.ShapeDtypeStruct(steered.shape, jnp.float32),
            jax.ShapeDtypeStruct((1, chosen.shape[0]), jnp.float32),
        ],
    )(steered, norm, chosen)


def body(
    base_inputs,
    small_inputs,
    base_norm_gain,
    base_query,
    base_keys_values,
    base_output,
    base_cache,
    base_final_gain,
    base_unembed,
    small_norm_gain,
    small_projections,
    small_output,
    small_cache,
    small_final_gain,
    small_unembed,
    lengths,
    next_tokens,
):
    row_count = lengths.shape[0]
    total_rows = STEPS * row_count
    vocab_width = base_unembed.shape[0]
    small_block = small_inputs.reshape(total_rows, -1)
    base_block = base_inputs.reshape(total_rows, -1)
    pair_weights = jnp.swapaxes(base_keys_values, 1, 2)
    steered, norm, chosen = whole_stage(
        small_block,
        base_block,
        small_norm_gain,
        base_norm_gain,
        small_final_gain,
        base_final_gain,
        lengths,
        next_tokens,
        small_projections,
        base_query,
        pair_weights,
        small_cache,
        base_cache,
        small_output,
        base_output,
        small_unembed,
        base_unembed,
    )
    log_probs, chosen = finish(steered, norm, chosen)
    return log_probs.reshape(STEPS, row_count, vocab_width), chosen.reshape(row_count)


def solution(mesh):
    placed = (
        P(None, "dp", ("grp", "tp")),
        P("grp", None, "dp", "tp"),
        P(),
        P(None, ("grp", "tp")),
        P(None, None, ("grp", "tp")),
        P(("grp", "tp"), None),
        P(None, "dp", ("grp", "tp"), None),
        P(),
        P(("grp", "tp"), None),
        P("grp", None),
        P("grp", None, None, "tp"),
        P("grp", "tp", None),
        P("grp", None, "dp", "tp", None),
        P("grp", None),
        P("grp", None, "tp", None),
        P("dp"),
        P(None, "dp"),
    )
    return jax.shard_map(
        body,
        mesh=mesh,
        in_specs=placed,
        out_specs=(P(None, "dp", ("grp", "tp")), P("dp")),
        check_vma=False,
    )
```

time: 324 us -> 133 us (0.41)
  waiting for transfers between devices: 74.9 us -> 0 us
  Pallas kernels: 168 us -> 132 us
  local copies, waits for them, and re-layouts: 28.8 us -> 0 us
  matrix products: 18.8 us -> 0 us
  other arithmetic: 15.3 us -> 0 us
  between operations: 14.3 us -> 0.65 us
    all_gather x2 -> x0, waiting for transfers between devices: 51.2 us -> none  [the longest x1 35.5 us: body(): small_full = lax.all_gather(small_block, 'tp', axis=0)]
    pallas_call x10 -> x2, Pallas kernels: 168 us -> 132 us  [the longest x1 130 us: whole_stage(): pl.pallas_call(functools.partial(whole_kernel, size, share, slots), in_sp...]
    dot_general x8 -> x0, matrix products: 18.8 us -> none  [the longest x1 8.07 us: body(): jnp.einsum('rhsl,rhdl->srhd', cached, values, preferred_element_type=jnp....]
    ppermute x3 -> x0, waiting for transfers between devices: 16.1 us -> none  [the longest x2 16.1 us: partner(): lax.ppermute(array, axis, [(i, i ^ 1 << bit) for i in range(lax.axis_size...]
    slice x6 -> x0, local copies, waits for them, and re-layouts: 14.4 us -> none  [the longest x1 11.7 us: body(): values = small_cache[0, 1].reshape(row_count, small_heads, HD, CACHE)]
    unnamed x40 -> x0, local copies, waits for them, and re-layouts: 9.72 us -> none
    reduce_scatter x1 -> x0, waiting for transfers between devices: 6.98 us -> none  [body(): lax.psum_scatter(small_partial, 'tp', scatter_dimension=0, tiled=False)]
    convert_element_type x8 -> x0, other arithmetic: 5.12 us -> none  [the longest x3 1.96 us: rotate(): return (values * cosine + other * sine).astype(jnp.bfloat16)]
  transfers between devices with their start and end apart: 6 -> 0, of which waited for: 4 -> 0; matrix products, arithmetic and copies ran while one was open for 10% -> 0% of each run, Pallas kernels for 41% -> 0%
where the time goes in v1:
time: 133 us
  Pallas kernels  132 us (99%)
    pallas_call x1, Pallas kernels, whole_stage(): pl.pallas_call(functools.partial(whole_kernel, size, share, slots), in_sp...  130 us

profile of v1, /device:TPU:0, one launch (start us, length us, event | category | flops | bytes accessed | tf_op | source)
XLA Modules:
  0.0 132.8 jit_solution(12944773683860519652)
XLA Ops:
  0.6 130.0 %shard_map.176 = (f32[192,1024]{1,0:T(8,128)}, f32[192,128]{1,0:T(8,128)}, f32[64,128]{1,0:T(8,128)}) custom-call(bf16[192,512]{1,0:T(8,128)(2,1)} %bitcast.10, bf16[192,512]{1,0:T(8,128)(2,1)} %bitcast.11, f32[8,1,512]{2,1,0:T(1,128)} %bitcast.14, f32[16,1,512]{2,1,0:T(1,128)} %bitcast.12, f32[8,1,512]{2,1,0:T(1,128)} %bitcast.15, f32[16,1,512]{2,1,0:T(1,128)} %bitcast.13, ...), custom_call_target="tpu_custom_call" | custom-call | tf_op jit(solution)/shard_map/pallas_call | solution.py:1306
  130.6 2.2 %shard_map.177 = (f32[192,1024]{1,0:T(8,128)}, f32[1,64]{1,0:T(1,128)}) custom-call(f32[192,1024]{1,0:T(8,128)} %get-tuple-element.7.steered, f32[192,128]{1,0:T(8,128)} %get-tuple-element.8.norm, f32[64,128]{1,0:T(8,128)} %get-tuple-element.9.chosen), custom_call_target="tpu_custom_call" | custom-call | tf_op jit(solution)/shard_map/pallas_call | solution.py:1398

commit v2 on v1

--- a/solution.py
+++ b/solution.py
@@ -15,7 +15,7 @@
 
 EPSILON = 1e-05
 NEGATIVE = -1e30
-VMEM_LIMIT = 60 * 1024 * 1024
+VMEM_LIMIT = 61 * 1024 * 1024
 LANES = 128
 
 
@@ -47,6 +47,8 @@
 def input_part(
     size,
     greet,
+    fetch_keys,
+    score,
     small_x,
     base_x,
     small_gain,
@@ -116,16 +118,11 @@
     slice_width = pair_w.shape[1]
     copies = LANES // slice_width
 
-    def pair_fetch(side, step, kind, copy):
+    def pair_fetch(side, step):
         columns = pl.ds(pl.multiple_of(base_source(side, step) * base_width, base_width), base_width)
         return pltpu.make_async_copy(
-            pair_w.at[kind, :, columns],
-            pair_tiles.at[side, step, pl.ds(kind * LANES + copy * slice_width, slice_width)],
-            pair_w_sems.at[side, step, kind * copies + copy],
-        )
-
-    def pair_fetches(side, step):
-        return [pair_fetch(side, step, kind, copy) for kind in range(2) for copy in range(copies)]
+            pair_w.at[:, :, columns], pair_tiles.at[side, step], pair_w_sems.at[side, step]
+        )
 
     keeps = [
         pltpu.make_async_copy(small_x, small_box.at[0], local_sems.at[0]),
@@ -138,11 +135,11 @@
         small_fetch(step).start()
         for side in range(2):
             query_fetch(side, step).start()
-            for fetch in pair_fetches(side, step):
-                fetch.start()
+            pair_fetch(side, step).start()
         return carry
 
     lax.fori_loop(0, size, fetch_all, 0)
+    fetch_keys()
     small_total[...] = jnp.zeros_like(small_total)
     query_total[...] = jnp.zeros_like(query_total)
     pair_total[...] = jnp.zeros_like(pair_total)
@@ -200,8 +197,8 @@
 
     def base_work(side, step):
         query_fetch(side, step).wait()
-        for fetch in pair_fetches(side, step):
-            fetch.wait()
+        pair_fetch(side, step).wait()
+        tile = [pair_tiles[side, step, kind] for kind in range(2) for copy in range(copies)]
         x = base_box[side, step].astype(jnp.float32)
         base_square[...] += square_lanes(x)
         scaled = (x * base_gain[base_source(side, step)]).astype(jnp.bfloat16)
@@ -210,16 +207,16 @@
         )
         pair_total[...] += lax.dot_general(
             scaled,
-            pair_tiles[side, step],
+            jnp.concatenate(tile, axis=0),
             (((1,), (1,)), ((), ())),
             preferred_element_type=jnp.float32,
         )
 
-    small_fore(0).start()
-    small_back(0).start()
     base_fore(0).start()
     base_back(0).start()
     core_hop(0).start()
+    small_fore(0).start()
+    small_back(0).start()
 
     def place(row, carry):
         small_cos[pl.ds(row, 1), :] = jnp.full((1, LANES), lengths[row].astype(jnp.float32))
@@ -246,16 +243,6 @@
     base_work(0, 0)
 
     def ring_step(step, carry):
-        small_fore(step - 1).wait_recv()
-        small_fore(step).start()
-        small_back(step - 1).wait_recv()
-
-        @pl.when(step < half - 1)
-        def _():
-            small_back(step).start()
-
-        small_work(step)
-        small_work(size - step)
         base_fore(step - 1).wait_recv()
         base_fore(step).start()
         base_back(step - 1).wait_recv()
@@ -268,6 +255,16 @@
         core_hop(size - step).start()
         base_work(0, step)
         base_work(0, size - step)
+        small_fore(step - 1).wait_recv()
+        small_fore(step).start()
+        small_back(step - 1).wait_recv()
+
+        @pl.when(step < half - 1)
+        def _():
+            small_back(step).start()
+
+        small_work(step)
+        small_work(size - step)
         core_hop(step - 1).wait_recv()
         base_work(1, step - 1)
 
@@ -284,32 +281,12 @@
     if half > 1:
         core_hop(half + 1).wait_recv()
         base_work(1, half + 1)
-    small_fore(half - 1).wait_recv()
-    small_work(half)
     base_fore(half - 1).wait_recv()
     core_hop(half).start()
     base_work(0, half)
     core_hop(half).wait_recv()
     base_work(1, half)
 
-    def settle(step, carry):
-        small_fore(step).wait_send()
-        base_fore(step).wait_send()
-        return carry
-
-    def settle_back(step, carry):
-        small_back(step).wait_send()
-        base_back(step).wait_send()
-        return carry
-
-    def settle_core(step, carry):
-        core_hop(step).wait_send()
-        return carry
-
-    lax.fori_loop(0, half, settle, 0)
-    lax.fori_loop(0, half - 1, settle_back, 0)
-    lax.fori_loop(0, size, settle_core, 0)
-
     def scale_of(square_ref, width):
         total = jnp.sum(square_ref[...], axis=-1, keepdims=True)
         return lax.rsqrt(total / width + EPSILON)
@@ -319,14 +296,6 @@
         rest = ref.shape[-2] - rows
         ref[index + (slice(rows, rows + rest),)] = jnp.zeros((rest, LANES), jnp.float32)
 
-    scale = scale_of(small_square, size * small_width)
-    for part in range(small_out.shape[0]):
-        for tile in range(small_out.shape[1]):
-            columns = slice(tile * LANES, (tile + 1) * LANES)
-            values = small_total[part, :, columns] * scale
-            if part < 2:
-                values = values * small_cos[...] + swap_pairs(values) * small_sin[...]
-            store(small_out, (part, tile), values)
     scale = scale_of(base_square, 2 * size * base_width)
     for tile in range(query_out.shape[0]):
         columns = slice(tile * LANES, (tile + 1) * LANES)
@@ -337,12 +306,39 @@
     values = values * base_cos[...] + swap_pairs(values) * base_sin[...]
     store(pair_out, (0,), values)
     store(pair_out, (1,), pair_total[:, LANES:] * scale)
+    score()
+    small_fore(half - 1).wait_recv()
+    small_work(half)
+    scale = scale_of(small_square, size * small_width)
+    for part in range(small_out.shape[0]):
+        for tile in range(small_out.shape[1]):
+            columns = slice(tile * LANES, (tile + 1) * LANES)
+            values = small_total[part, :, columns] * scale
+            if part < 2:
+                values = values * small_cos[...] + swap_pairs(values) * small_sin[...]
+            store(small_out, (part, tile), values)
+
+    def settle(step, carry):
+        small_fore(step).wait_send()
+        base_fore(step).wait_send()
+        return carry
+
+    def settle_back(step, carry):
+        small_back(step).wait_send()
+        base_back(step).wait_send()
+        return carry
+
+    def settle_core(step, carry):
+        core_hop(step).wait_send()
+        return carry
+
+    lax.fori_loop(0, half, settle, 0)
+    lax.fori_loop(0, half - 1, settle_back, 0)
+    lax.fori_loop(0, size, settle_core, 0)
 
 
 def attention_part(
     share,
-    begin,
-    between,
     small_qkv,
     query,
     pair,
@@ -352,9 +348,7 @@
     small_out,
     base_out,
     small_keys,
-    small_values,
     base_keys,
-    base_values,
     small_scores,
     small_fresh,
     small_weights,
@@ -385,33 +379,30 @@
     def peer(step):
         return (group, near + (mine % share + step) % share, data)
 
-    def small_fetch(kind, index):
+    def small_fetch(kind, index, target):
         rows = pl.ds(index * chunk, chunk)
-        target = (small_keys, small_values)[kind]
         return pltpu.make_async_copy(
             small_cache.at[0, kind, rows], target.at[rows], small_sems.at[kind, index]
         )
 
-    def base_fetch(kind, copy):
-        target = (base_keys, base_values)[kind]
+    def base_fetch(kind, copy, target):
         return pltpu.make_async_copy(
             base_cache.at[kind],
             target.at[:, pl.ds(copy * slice_width, slice_width)],
             base_sems.at[kind, copy],
         )
 
-    for copy in range(copies):
-        base_fetch(0, copy).start()
-    for kind in range(2):
-
-        def fetch(index, carry, kind=kind):
-            small_fetch(kind, index).start()
+    def fetch_small(kind, target):
+        def fetch(index, carry):
+            small_fetch(kind, index, target).start()
             return carry
 
         lax.fori_loop(0, chunks, fetch, 0)
-    for copy in range(copies):
-        base_fetch(1, copy).start()
-    begin()
+
+    def fetch_keys():
+        for copy in range(copies):
+            base_fetch(0, copy, base_keys).start()
+        fetch_small(0, small_keys)
 
     def four(ref, row):
         return ref[pl.ds(row, 4, stride=row_count), :]
@@ -439,9 +430,6 @@
     fresh_masks = [
         lanes & (lane % 8 <= step_of) & (lane % 8 < STEPS) for lanes in fresh_lanes
     ]
-
-    for copy in range(copies):
-        base_fetch(0, copy).wait()
 
     def base_left(r):
         tiles = [four(query.at[g // copies], r) for g in range(base_rows // 4)]
@@ -470,7 +458,6 @@
             share_copy(step, index).start()
         return carry
 
-    lax.fori_loop(0, chunks, base_score, 0)
 
     depth = small_keys.shape[1]
     small_row = lax.broadcasted_iota(jnp.int32, (part_rows, depth), 0)
@@ -494,7 +481,7 @@
         return left.astype(jnp.bfloat16)
 
     def small_score(index, carry):
-        small_fetch(0, index).wait()
+        small_fetch(0, index, small_keys).wait()
         for inner in range(0, chunk, 2):
             r = index * chunk + inner
             left = jnp.concatenate([small_left(r), small_left(r + 1)], axis=0)
@@ -508,7 +495,10 @@
                 small_fresh[r + odd] = fresh[rows]
         return carry
 
-    lax.fori_loop(0, chunks, small_score, 0)
+    def score():
+        for copy in range(copies):
+            base_fetch(0, copy, base_keys).wait()
+        lax.fori_loop(0, chunks, base_score, 0)
 
     def small_softmax(index, carry):
         for inner in range(chunk):
@@ -527,104 +517,113 @@
             small_fresh_weights[r] = (fresh / total).astype(jnp.bfloat16).astype(jnp.float32)
         return carry
 
-    lax.fori_loop(0, chunks, small_softmax, 0)
-
-    def small_value(index, carry):
-        small_fetch(1, index).wait()
-        for inner in range(0, chunk, 2):
-            r = index * chunk + inner
-            none = jnp.zeros((part_rows, CACHE), jnp.bfloat16)
-            first = jnp.concatenate([small_weights[r], none], axis=1)
-            second = jnp.concatenate([none, small_weights[r + 1]], axis=1)
-            left = jnp.concatenate([first, second], axis=0)
-            values = jnp.concatenate([small_values[r], small_values[r + 1]], axis=1)
-            both = nt(left, values)
-            for odd in range(2):
-                fresh_values = heads_of(2, r + odd, 1)
-                weights = small_fresh_weights[r + odd]
-                for head in range(depth // HD):
-                    columns = slice(head * HD, (head + 1) * HD)
-                    rows = slice(4 * head, 4 * head + 4)
-                    total = both[odd * part_rows + 4 * head : odd * part_rows + 4 * head + 4, columns]
-                    for n in range(STEPS):
-                        total = total + (
-                            weights[rows, 4 * odd + n : 4 * odd + n + 1]
-                            * fresh_values[n : n + 1, columns]
-                        )
-                    small_result[head, pl.ds(r + odd, 4, stride=row_count), :] = total
-        return carry
-
-    lax.fori_loop(0, chunks, small_value, 0)
-    rows = small_out.shape[0]
-    for head in range(depth // HD):
-        small_out[:, head * HD : (head + 1) * HD] = small_result[head, :rows].astype(small_out.dtype)
-
-    between()
-    for copy in range(copies):
-        base_fetch(1, copy).wait()
-
-    def base_softmax(r, odd):
-        scores = base_scores[r]
-        for step in range(share - 1):
-            scores = scores + base_land[step, r].astype(jnp.float32)
-        fresh = jnp.where(
-            step_of == 0,
-            pltpu.roll(scores, base_rows - 3, 0),
-            jnp.where(
-                step_of == 1,
-                pltpu.roll(scores, base_rows - 2, 0),
-                pltpu.roll(scores, base_rows - 1, 0),
-            ),
-        )
-        cached = jnp.where(lane < lengths[r], scores * factor, NEGATIVE)
-        fresh = jnp.where(fresh_masks[odd], fresh * factor, NEGATIVE)
-        row_max = jnp.max(jnp.maximum(cached, fresh), axis=-1, keepdims=True)
-        cached = jnp.exp(cached - row_max)
-        fresh = jnp.exp(fresh - row_max)
-        total = jnp.sum(cached + fresh, axis=-1, keepdims=True)
-        return (cached / total).astype(jnp.bfloat16), (fresh / total).astype(jnp.bfloat16)
-
-    def base_value(index, carry):
-        for step in range(1, share):
-            share_copy(step, index).wait_recv()
-        for inner in range(0, chunk, 2):
-            r = index * chunk + inner
-            none = jnp.zeros((base_rows, CACHE), jnp.bfloat16)
-            cached, fresh = zip(base_softmax(r, 0), base_softmax(r + 1, 1))
-            first = jnp.concatenate([cached[0], none], axis=1)
-            second = jnp.concatenate([none, cached[1]], axis=1)
-            left = jnp.concatenate([first, second], axis=0)
-            values = jnp.concatenate([base_values[r], base_values[r + 1]], axis=1)
-            both = nt(left, values) + jnp.dot(
-                jnp.concatenate(fresh, axis=0),
-                fresh_rows(pair.at[1], r),
-                preferred_element_type=jnp.float32,
+
+    def finish(begin, between, small_values, base_values):
+        fetch_small(1, small_values)
+        for copy in range(copies):
+            base_fetch(1, copy, base_values).start()
+        begin()
+        lax.fori_loop(0, chunks, small_score, 0)
+        lax.fori_loop(0, chunks, small_softmax, 0)
+
+        def small_value(index, carry):
+            small_fetch(1, index, small_values).wait()
+            for inner in range(0, chunk, 2):
+                r = index * chunk + inner
+                none = jnp.zeros((part_rows, CACHE), jnp.bfloat16)
+                first = jnp.concatenate([small_weights[r], none], axis=1)
+                second = jnp.concatenate([none, small_weights[r + 1]], axis=1)
+                left = jnp.concatenate([first, second], axis=0)
+                values = jnp.concatenate([small_values[r], small_values[r + 1]], axis=1)
+                both = nt(left, values)
+                for odd in range(2):
+                    fresh_values = heads_of(2, r + odd, 1)
+                    weights = small_fresh_weights[r + odd]
+                    for head in range(depth // HD):
+                        columns = slice(head * HD, (head + 1) * HD)
+                        rows = slice(4 * head, 4 * head + 4)
+                        total = both[odd * part_rows + 4 * head : odd * part_rows + 4 * head + 4, columns]
+                        for n in range(STEPS):
+                            total = total + (
+                                weights[rows, 4 * odd + n : 4 * odd + n + 1]
+                                * fresh_values[n : n + 1, columns]
+                            )
+                        small_result[head, pl.ds(r + odd, 4, stride=row_count), :] = total
+            return carry
+
+        lax.fori_loop(0, chunks, small_value, 0)
+        rows = small_out.shape[0]
+        for head in range(depth // HD):
+            small_out[:, head * HD : (head + 1) * HD] = small_result[head, :rows].astype(small_out.dtype)
+
+        between()
+        for copy in range(copies):
+            base_fetch(1, copy, base_values).wait()
+
+        def base_softmax(r, odd):
+            scores = base_scores[r]
+            for step in range(share - 1):
+                scores = scores + base_land[step, r].astype(jnp.float32)
+            fresh = jnp.where(
+                step_of == 0,
+                pltpu.roll(scores, base_rows - 3, 0),
+                jnp.where(
+                    step_of == 1,
+                    pltpu.roll(scores, base_rows - 2, 0),
+                    pltpu.roll(scores, base_rows - 1, 0),
+                ),
             )
-            for odd in range(2):
-                heads = both[odd * base_rows : (odd + 1) * base_rows]
-                for tile in range(base_out.shape[1] // LANES):
-                    g = tile * copies
-                    part = heads[4 * g : 4 * g + 4]
-                    for copy in range(1, copies):
-                        g = tile * copies + copy
-                        part = jnp.where(
-                            lane[:4] // slice_width == copy, heads[4 * g : 4 * g + 4], part
-                        )
-                    base_result[tile, pl.ds(r + odd, 4, stride=row_count), :] = part
-        return carry
-
-    lax.fori_loop(0, chunks, base_value, 0)
-    for tile in range(base_out.shape[1] // LANES):
-        base_out[:, tile * LANES : (tile + 1) * LANES] = base_result[tile, :rows].astype(
-            base_out.dtype
-        )
-
-    def settle(index, carry):
-        for step in range(1, share):
-            share_copy(step, index).wait_send()
-        return carry
-
-    lax.fori_loop(0, chunks, settle, 0)
+            cached = jnp.where(lane < lengths[r], scores * factor, NEGATIVE)
+            fresh = jnp.where(fresh_masks[odd], fresh * factor, NEGATIVE)
+            row_max = jnp.max(jnp.maximum(cached, fresh), axis=-1, keepdims=True)
+            cached = jnp.exp(cached - row_max)
+            fresh = jnp.exp(fresh - row_max)
+            total = jnp.sum(cached + fresh, axis=-1, keepdims=True)
+            return (cached / total).astype(jnp.bfloat16), (fresh / total).astype(jnp.bfloat16)
+
+        def base_value(index, carry):
+            for step in range(1, share):
+                share_copy(step, index).wait_recv()
+            for inner in range(0, chunk, 2):
+                r = index * chunk + inner
+                none = jnp.zeros((base_rows, CACHE), jnp.bfloat16)
+                cached, fresh = zip(base_softmax(r, 0), base_softmax(r + 1, 1))
+                first = jnp.concatenate([cached[0], none], axis=1)
+                second = jnp.concatenate([none, cached[1]], axis=1)
+                left = jnp.concatenate([first, second], axis=0)
+                values = jnp.concatenate([base_values[r], base_values[r + 1]], axis=1)
+                both = nt(left, values) + jnp.dot(
+                    jnp.concatenate(fresh, axis=0),
+                    fresh_rows(pair.at[1], r),
+                    preferred_element_type=jnp.float32,
+                )
+                for odd in range(2):
+                    heads = both[odd * base_rows : (odd + 1) * base_rows]
+                    for tile in range(base_out.shape[1] // LANES):
+                        g = tile * copies
+                        part = heads[4 * g : 4 * g + 4]
+                        for copy in range(1, copies):
+                            g = tile * copies + copy
+                            part = jnp.where(
+                                lane[:4] // slice_width == copy, heads[4 * g : 4 * g + 4], part
+                            )
+                        base_result[tile, pl.ds(r + odd, 4, stride=row_count), :] = part
+            return carry
+
+        lax.fori_loop(0, chunks, base_value, 0)
+        for tile in range(base_out.shape[1] // LANES):
+            base_out[:, tile * LANES : (tile + 1) * LANES] = base_result[tile, :rows].astype(
+                base_out.dtype
+            )
+
+        def settle(index, carry):
+            for step in range(1, share):
+                share_copy(step, index).wait_send()
+            return carry
+
+        lax.fori_loop(0, chunks, settle, 0)
+
+    return fetch_keys, score, finish
 
 
 def output_part(
@@ -854,10 +853,6 @@
                 base_t_sems.at[side, use],
             )
 
-        for step in range(min(slots, size)):
-            small_fetch(step).start()
-            base_fetch(0, step).start()
-            base_fetch(1, step).start()
         core_send(half)
         if half > 1:
             core_send(half - 1)
@@ -866,6 +861,10 @@
             base_send(half - 1, behind, None)
             core_send(half + 1)
             core_send(half - 2)
+        for step in range(min(slots, size)):
+            small_fetch(step).start()
+            base_fetch(0, step).start()
+            base_fetch(1, step).start()
 
         def sum_step(step, carry):
             small_send(half + step, ahead, half + step - 1)
@@ -1149,116 +1148,122 @@
         lax.fori_loop(1, count, call, 0)
         pl.semaphore_wait(barrier, count - 1)
 
-    def first(small_tiles, query_tiles, pair_tiles, small_total, query_total, pair_total, *tables):
-        input_part(
-            size,
-            greet,
-            small_x,
-            base_x,
-            small_gain,
-            base_gain,
-            small_w,
-            query_w,
-            pair_w,
-            lengths,
+    cache = pltpu.VMEM((row_count, depth, CACHE), half)
+    wide = pltpu.VMEM((row_count, LANES, CACHE), half)
+    slice_width = pair_w.shape[1]
+
+    def outer(small_keys, base_keys):
+        fetch_keys, score, attend = attention_part(
+            share,
             small_qkv,
             query,
             pair,
-            small_box,
-            base_box,
-            small_tiles,
-            query_tiles,
-            pair_tiles,
-            small_total,
-            query_total,
-            pair_total,
-            small_square,
-            base_square,
-            *tables,
-            *input_sems,
-        )
-
-    table = pltpu.VMEM((rows, LANES), jnp.float32)
-    pl.run_scoped(
-        first,
-        pltpu.VMEM((size, parts, small_width, depth), half),
-        pltpu.VMEM((2, size, base_width, query_w.shape[1]), half),
-        pltpu.VMEM((2, size, 2 * LANES, base_width), half),
-        pltpu.VMEM((parts, rows, depth), jnp.float32),
-        pltpu.VMEM((rows, query_w.shape[1]), jnp.float32),
-        pltpu.VMEM((rows, 2 * LANES), jnp.float32),
-        table,
-        table,
-        table,
-        table,
-    )
-    def after(small_w_tiles, base_w_tiles):
-        begin, start_small, rest = output_part(
-            size,
+            lengths,
+            small_cache,
+            base_cache,
             small_heads,
             base_heads,
-            small_final,
-            base_final,
-            next_tokens,
-            small_out_w,
-            base_out_w,
-            small_table,
-            base_table,
-            steered,
-            norm,
-            chosen,
-            small_w_tiles,
-            base_w_tiles,
-            *output_scratch[:6],
-            small_box,
-            base_box,
-            *output_scratch[6:9],
-            small_square,
-            base_square,
-            *output_scratch[9:],
-            *output_sems,
-        )
-
-        def between():
-            start_small()
-
-        def second(small_keys, small_values, base_keys, base_values):
-            attention_part(
-                share,
-                begin,
-                between,
+            small_keys,
+            base_keys,
+            *attention_scratch,
+            attention_scratch[-1],
+            *attention_sems,
+        )
+
+        def first(small_tiles, query_tiles, pair_tiles, small_total, query_total, pair_total, *tables):
+            input_part(
+                size,
+                greet,
+                fetch_keys,
+                score,
+                small_x,
+                base_x,
+                small_gain,
+                base_gain,
+                small_w,
+                query_w,
+                pair_w,
+                lengths,
                 small_qkv,
                 query,
                 pair,
-                lengths,
-                small_cache,
-                base_cache,
+                small_box,
+                base_box,
+                small_tiles,
+                query_tiles,
+                pair_tiles,
+                small_total,
+                query_total,
+                pair_total,
+                small_square,
+                base_square,
+                *tables,
+                *input_sems,
+            )
+
+        table = pltpu.VMEM((rows, LANES), jnp.float32)
+        pl.run_scoped(
+            first,
+            pltpu.VMEM((size, parts, small_width, depth), half),
+            pltpu.VMEM((2, size, base_width, query_w.shape[1]), half),
+            pltpu.VMEM((2, size, 2, slice_width, base_width), half),
+            pltpu.VMEM((parts, rows, depth), jnp.float32),
+            pltpu.VMEM((rows, query_w.shape[1]), jnp.float32),
+            pltpu.VMEM((rows, 2 * LANES), jnp.float32),
+            table,
+            table,
+            table,
+            table,
+        )
+        def after(small_w_tiles, base_w_tiles):
+            begin, start_small, rest = output_part(
+                size,
                 small_heads,
                 base_heads,
-                small_keys,
-                small_values,
-                base_keys,
-                base_values,
-                *attention_scratch,
-                *attention_sems,
+                small_final,
+                base_final,
+                next_tokens,
+                small_out_w,
+                base_out_w,
+                small_table,
+                base_table,
+                steered,
+                norm,
+                chosen,
+                small_w_tiles,
+                base_w_tiles,
+                *output_scratch[:6],
+                small_box,
+                base_box,
+                *output_scratch[6:9],
+                small_square,
+                base_square,
+                *output_scratch[9:],
+                *output_sems,
             )
 
-        cache = pltpu.VMEM((row_count, depth, CACHE), half)
-        wide = pltpu.VMEM((row_count, LANES, CACHE), half)
-        pl.run_scoped(second, cache, cache, wide, wide)
-        vocab = base_table.shape[0]
+            def between():
+                start_small()
+
+            def second(small_values, base_values):
+                attend(begin, between, small_values, base_values)
+
+            pl.run_scoped(second, cache, wide)
+            vocab = base_table.shape[0]
+            pl.run_scoped(
+                rest,
+                pltpu.VMEM((slots, 2, vocab, small_width), half),
+                pltpu.VMEM((2, slots, vocab, base_width), half),
+            )
+
+        output_depth = base_out_w.shape[0]
         pl.run_scoped(
-            rest,
-            pltpu.VMEM((slots, 2, vocab, small_width), half),
-            pltpu.VMEM((2, slots, vocab, base_width), half),
-        )
-
-    output_depth = base_out_w.shape[0]
-    pl.run_scoped(
-        after,
-        pltpu.VMEM((size, depth, small_width), half),
-        pltpu.VMEM((2, size, output_depth, base_width), half),
-    )
+            after,
+            pltpu.VMEM((size, depth, small_width), half),
+            pltpu.VMEM((2, size, output_depth, base_width), half),
+        )
+
+    pl.run_scoped(outer, cache, wide)
 
 
 def whole_stage(
@@ -1322,7 +1327,7 @@
             space((rows, LANES), wide),
             space((rows, depth), half),
             space((rows, base_depth), half),
-            [dma((2,)), dma((size,)), dma((2, size)), dma((2, size, 2 * copies))]
+            [dma((2,)), dma((size,)), dma((2, size)), dma((2, size))]
             + [dma((size,))] * 6,
             [
                 space((row_count, part_rows, CACHE), wide),
@@ -1332,8 +1337,7 @@
                 space((row_count, base_rows, CACHE), wide),
                 space((row_count, base_rows, CACHE), half),
                 space((share - 1, row_count, base_rows, CACHE), half),
-                space((depth // LANES, padded, LANES), wide),
-                space((base_depth // LANES, padded, LANES), wide),
+                space((max(depth, base_depth) // LANES, padded, LANES), wide),
             ],
             [dma((2, chunks)), dma((2, copies)), dma((share - 1, chunks)), dma((share - 1, chunks))],
             [space((size, rows, small_width), half)] * 2
@@ -1390,15 +1394,25 @@
 
 def finish_kernel(steered, norm, chosen, log_out, chosen_out):
     log_out[...] = steered[...] - norm[:, :1]
-    chosen_out[...] = chosen[...].T[1:2]
+
+    @pl.when(pl.program_id(0) == 0)
+    def _():
+        chosen_out[...] = chosen[...].T[1:2]
 
 
 def finish(steered, norm, chosen):
-    whole = pl.BlockSpec(memory_space=pltpu.VMEM)
+    rows, width = steered.shape
+    tile = rows // STEPS
+    tall = pl.BlockSpec((tile, width), lambda i: (i, 0))
     return pl.pallas_call(
         finish_kernel,
-        in_specs=[whole] * 3,
-        out_specs=[whole] * 2,
+        grid=(STEPS,),
+        in_specs=[
+            tall,
+            pl.BlockSpec((tile, LANES), lambda i: (i, 0)),
+            pl.BlockSpec(chosen.shape, lambda i: (0, 0)),
+        ],
+        out_specs=[tall, pl.BlockSpec((1, chosen.shape[0]), lambda i: (0, 0))],
         out_shape=[
             jax.ShapeDtypeStruct(steered.shape, jnp.float32),
             jax.ShapeDtypeStruct((1, chosen.shape[0]), jnp.float32),

time: 133 us -> 129 us (0.970)
  Pallas kernels: 132 us -> 129 us
    pallas_call x1, Pallas kernels: 130 us -> 126 us  [whole_stage(): pl.pallas_call(functools.partial(whole_kernel, size, share, slots), in_sp...]
where the time goes in v2:
time: 129 us
  Pallas kernels  129 us (100%)
    pallas_call x1, Pallas kernels, whole_stage(): pl.pallas_call(functools.partial(whole_kernel, size, share, slots), in_sp...  126 us
    pallas_call x1, Pallas kernels, finish(): pl.pallas_call(finish_kernel, grid=(STEPS,), in_specs=[tall, pl.BlockSpec...  3.02 us

profile of v2, /device:TPU:0, one launch (start us, length us, event | category | flops | bytes accessed | tf_op | source)
XLA Modules:
  0.0 129.2 jit_solution(12878832150047714595)
XLA Ops:
  0.6 125.6 %shard_map.176 = (f32[192,1024]{1,0:T(8,128)}, f32[192,128]{1,0:T(8,128)}, f32[64,128]{1,0:T(8,128)}) custom-call(bf16[192,512]{1,0:T(8,128)(2,1)} %bitcast.10, bf16[192,512]{1,0:T(8,128)(2,1)} %bitcast.11, f32[8,1,512]{2,1,0:T(1,128)} %bitcast.14, f32[16,1,512]{2,1,0:T(1,128)} %bitcast.12, f32[8,1,512]{2,1,0:T(1,128)} %bitcast.15, f32[16,1,512]{2,1,0:T(1,128)} %bitcast.13, ...), custom_call_target="tpu_custom_call" | custom-call | tf_op jit(solution)/shard_map/pallas_call | solution.py:1311
  126.2 3.0 %shard_map.177 = (f32[192,1024]{1,0:T(8,128)}, f32[1,64]{1,0:T(1,128)}) custom-call(f32[192,1024]{1,0:T(8,128)} %get-tuple-element.7.steered, f32[192,128]{1,0:T(8,128)} %get-tuple-element.8.norm, f32[64,128]{1,0:T(8,128)} %get-tuple-element.9.chosen), custom_call_target="tpu_custom_call" | custom-call | tf_op jit(solution)/shard_map/pallas_call | solution.py:1407
